TPU v7x, 32 devices: a whole 2x2x4 slice. The times are simulated.
32 devices in a mesh: row: 4 (over x, core), col: 8 (over z, y).
Axes of the slice: x: 2, y: 2, z: 4, core: 2. Of those that a mesh axis runs over, the one named last changes fastest.
Arguments:
- images: bfloat16 [64, 197, 384], P(('row', 'col')), may hold values from -6 to 6
- counts: int32 [32], replicated, may hold values from 1 to 2, 48 in all
- upstream: bfloat16 [64, 197, 384], P(('row', 'col')), may hold values from -6 to 6
- qkv_weight: float32 [442368], P(('row', 'col')), may hold values from -3 to 3, as said below
- out_weight: float32 [147456], P(('row', 'col')), may hold values from -1.75 to 1.75
- fc1_weight: float32 [589824], P(('row', 'col')), may hold values from -0.3125 to 0.3125
- fc2_weight: float32 [589824], P(('row', 'col')), may hold values from -0.15625 to 0.15625
- gains: float32 [768], P(('row', 'col')), may hold values from 0.1 to 1.9
- biases: float32 [3840], P(('row', 'col')), may hold values from -2 to 2
- first_qkv: float32 [442368], P(('row', 'col')), may hold values from -32 to 32
- first_out: float32 [147456], P(('row', 'col')), may hold values from -6 to 6
- first_fc1: float32 [589824], P(('row', 'col')), may hold values from -56 to 56
- first_fc2: float32 [589824], P(('row', 'col')), may hold values from -128 to 128
- first_gains: float32 [768], P(('row', 'col')), may hold values from -192 to 192
- first_biases: float32 [3840], P(('row', 'col')), may hold values from -96 to 96
- second_qkv: float32 [442368], P(('row', 'col')), may hold values from 67 to 667
- second_out: float32 [147456], P(('row', 'col')), may hold values from 13 to 67
- second_fc1: float32 [589824], P(('row', 'col')), may hold values from 170 to 830
- second_fc2: float32 [589824], P(('row', 'col')), may hold values from 830 to 4000
- second_gains: float32 [768], P(('row', 'col')), may hold values from 1700 to 8300
- second_biases: float32 [3840], P(('row', 'col')), may hold values from 330 to 6700
Outputs:
- block_out: bfloat16 [64, 197, 384], P(('row', 'col'))
- images_grad: bfloat16 [64, 197, 384], P(('row', 'col'))
- qkv_weight_grad: float32 [442368], P(('row', 'col'))
- out_weight_grad: float32 [147456], P(('row', 'col'))
- fc1_weight_grad: float32 [589824], P(('row', 'col'))
- fc2_weight_grad: float32 [589824], P(('row', 'col'))
- gains_grad: float32 [768], P(('row', 'col'))
- biases_grad: float32 [3840], P(('row', 'col'))
- qkv_weight_new: float32 [442368], P(('row', 'col'))
- out_weight_new: float32 [147456], P(('row', 'col'))
- fc1_weight_new: float32 [589824], P(('row', 'col'))
- fc2_weight_new: float32 [589824], P(('row', 'col'))
- gains_new: float32 [768], P(('row', 'col'))
- biases_new: float32 [3840], P(('row', 'col'))
- first_qkv_new: float32 [442368], P(('row', 'col'))
- first_out_new: float32 [147456], P(('row', 'col'))
- first_fc1_new: float32 [589824], P(('row', 'col'))
- first_fc2_new: float32 [589824], P(('row', 'col'))
- first_gains_new: float32 [768], P(('row', 'col'))
- first_biases_new: float32 [3840], P(('row', 'col'))
- second_qkv_new: float32 [442368], P(('row', 'col'))
- second_out_new: float32 [147456], P(('row', 'col'))
- second_fc1_new: float32 [589824], P(('row', 'col'))
- second_fc2_new: float32 [589824], P(('row', 'col'))
- second_gains_new: float32 [768], P(('row', 'col'))
- second_biases_new: float32 [3840], P(('row', 'col'))
Inputs may be any that keep to these rules, and one draw needn't show every extreme that they name: `counts`: each device's entry is the number of its 2 image slots that hold images, the first ones; the entries sum to 48, and some device holds 2. `qkv_weight`: a dense projection matrix.
All inputs are finite; a program needn't handle non-finite values.
Results may differ from a plain program's by a relative error of at most 0.012.
The roundings to bfloat16 on the way count: a program that leaves them out, or rounds other values in their place, can miss the bound.
Values may be sent and summed in bfloat16 or wider, within the bound.
No kernel may reach another device: no remote copies, remote signals or barrier semaphores. Data moves between devices by JAX's collectives and lax.ppermute only.
A program may use at most 128 MiB of HBM per device.

v0:
```python
import functools
import math

import jax
import jax.numpy as jnp
from jax import lax
from jax.experimental import pallas as pl
from jax.experimental.pallas import tpu as pltpu
from jax.sharding import PartitionSpec as P

D = 384
HEADS = 6
HEAD_DIM = 64
FF = 1536
SEQ = 197
ADAM_STEP = 3

NORM_EPS = 1e-06
BETA_ONE = 0.9
BETA_TWO = 0.95
ADAM_EPS = 1e-08
DECAY_RATE = 0.1
RATES = (0.01, 0.05, 0.01, 0.01, 0.2, 0.2)
DECAYED = (True, True, True, True, False, False)
INV_ROOT_TWO = 0.7071067811865476
INV_ROOT_TWOPI = 0.3989422804014327

AXES = ("row", "col")
F32 = jnp.float32
BF16 = jnp.bfloat16
LANES = 128
PAD = 208
IMGS = 2
ROWS = IMGS * PAD
BLOCKS = 32
STRIPE = D // BLOCKS
QKV_TILES = 3 * D // LANES
OUT_TILES = D // LANES
FC_TILES = FF // LANES
QKV_ROWS = STRIPE * QKV_TILES
OUT_ROWS = STRIPE * OUT_TILES
FC_ROWS = STRIPE * FC_TILES
TALL = FF // BLOCKS
BIAS_ROW = QKV_ROWS
GAIN_ROW = BIAS_ROW + 1
FIRST_ROWS = 112
SECOND_SPLIT = (160, 176)
SECOND_ROWS = sum(SECOND_SPLIT)
OUT_START = FC_ROWS
FC2_START = OUT_START + OUT_ROWS
GAINS = 2 * D
BIASES = 6 * D + FF
GAIN_PART = GAINS // BLOCKS
BIAS_PART = BIASES // BLOCKS
CHUNKS = FF // D
Y_BIT, Z_LOW, Z_HIGH, CORE_BIT, X_BIT = 1, 2, 4, 8, 16


def nn(a, b):
    return jnp.dot(a, b, preferred_element_type=F32)


def nt(a, b):
    return lax.dot_general(a, b, (((1,), (1,)), ((), ())), preferred_element_type=F32)


def tn(a, b):
    return lax.dot_general(a, b, (((0,), (0,)), ((), ())), preferred_element_type=F32)


def norm_forward(row_data):
    centered = row_data - jnp.mean(row_data, axis=-1, keepdims=True)
    inv_std = lax.rsqrt(jnp.mean(centered * centered, axis=-1, keepdims=True) + NORM_EPS)
    return (centered * inv_std, inv_std)


def norm_backward(grad_hat, normed, inv_std):
    return inv_std * (
        grad_hat
        - jnp.mean(grad_hat, axis=-1, keepdims=True)
        - normed * jnp.mean(grad_hat * normed, axis=-1, keepdims=True)
    )


def masks_of(index, color):
    return (index & 3) * Z_LOW + (index >> 2) * (Y_BIT if color == 0 else X_BIT)


def variants(color):
    last = X_BIT if color == 0 else Y_BIT
    return (0, last, CORE_BIT, last + CORE_BIT)


def unpack(me, piece_refs, flat_ref, color, start, count):
    for piece_ref, extra in zip(piece_refs, variants(color)):

        def body(i, carry, piece_ref=piece_ref, extra=extra):
            owner = me ^ (masks_of(i, color) ^ extra)
            flat_ref[owner, start : start + count, :] = piece_ref[i].astype(F32)
            return carry

        lax.fori_loop(0, 8, body, 0)


def pack(me, grad_ref, out_refs, color, start, count):
    for out_ref, extra in zip(out_refs, variants(color)):

        def body(i, carry, out_ref=out_ref, extra=extra):
            owner = me ^ (masks_of(i, color) ^ extra)
            out_ref[i] = grad_ref[owner, start : start + count, :].astype(BF16)
            return carry

        lax.fori_loop(0, 8, body, 0)


def striped_rows(flat_ref, quad, start, stride):
    parts = [flat_ref[4 * quad + u, pl.ds(start, STRIPE, stride=stride), :] for u in range(4)]
    return jnp.concatenate(parts, axis=0).astype(BF16)


def scatter_rows(flat_ref, pair, start, stride, value):
    for u in range(2):
        flat_ref[2 * pair + u, pl.ds(start, STRIPE, stride=stride), :] = value[
            u * STRIPE : (u + 1) * STRIPE
        ]


def select_matrix(part, total):
    lane = lax.broadcasted_iota(jnp.int32, (LANES, total), 1)
    sub = lax.broadcasted_iota(jnp.int32, (LANES, total), 0)
    block = (lane * ((1 << 22) // part + 1)) >> 22
    return jnp.where(lane - block * part == sub, 1.0, 0.0).astype(BF16)


def owner_mask(part, total):
    lane = lax.broadcasted_iota(jnp.int32, (BLOCKS, total), 1)
    block = lax.broadcasted_iota(jnp.int32, (BLOCKS, total), 0)
    return (lane >= block * part) & (lane < block * part + part)


def spread(block_rows, part, total):
    moved = nn(block_rows.astype(BF16), select_matrix(part, total))
    return jnp.sum(jnp.where(owner_mask(part, total), moved, 0.0), axis=0, keepdims=True)


def collect(row, part, total):
    own = jnp.where(owner_mask(part, total), jnp.broadcast_to(row, (BLOCKS, total)), 0.0)
    return nt(own.astype(BF16), select_matrix(part, total))


def load_padded(x_ref, padded_ref, scales=None):
    for b in range(IMGS):
        tail = (SEQ // 16) * 16
        padded_ref[b * PAD + tail : (b + 1) * PAD, :] = jnp.zeros((PAD - tail, D), F32)
        value = x_ref[b].astype(F32)
        if scales is not None:
            value = value * scales[b]
        padded_ref[b * PAD : b * PAD + SEQ, :] = value


def bias_slice(vec_ref, start, size):
    return vec_ref[:, GAINS + start : GAINS + start + size]


def head_masks():
    lane = lax.broadcasted_iota(jnp.int32, (1, LANES), 1)
    low = jnp.where(lane < HEAD_DIM, 1.0, 0.0)
    return (low.astype(BF16), (1.0 - low).astype(BF16))


def position(swaps):
    return lax.axis_index(AXES) if swaps else jnp.int32(0)


def attend_kernel(swaps, counts_ref, x_ref, *refs):
    pieces = refs[:4]
    wqkv_ref, vec_ref, qkv_ref, att_ref = refs[4:8]
    flat_ref, pad_ref = refs[8:]
    me = position(swaps)
    unpack(me, pieces, flat_ref, 0, 0, FIRST_ROWS)

    def quads(quad, carry):
        rows = pl.ds(pl.multiple_of(quad * 4 * STRIPE, 16), 4 * STRIPE)
        for t in range(QKV_TILES):
            wqkv_ref[rows, t * LANES : (t + 1) * LANES] = striped_rows(
                flat_ref, quad, t, QKV_TILES
            )
        return carry

    lax.fori_loop(0, BLOCKS // 4, quads, 0)
    vec_ref[:, :GAINS] = spread(flat_ref[:, GAIN_ROW, :], GAIN_PART, GAINS)
    vec_ref[:, GAINS:] = spread(flat_ref[:, BIAS_ROW, :], BIAS_PART, BIASES)

    load_padded(x_ref, pad_ref)
    hat_in, _ = norm_forward(pad_ref[...])
    normed_in = (hat_in * vec_ref[:, :D] + bias_slice(vec_ref, 0, D)).astype(BF16)
    qkv_ref[:, :D] = (
        nn(normed_in, wqkv_ref[:, :D]) + bias_slice(vec_ref, D, D)
    ).astype(BF16)
    qkv_ref[:, D : 2 * D] = nn(normed_in, wqkv_ref[:, D : 2 * D]).astype(BF16)
    qkv_ref[:, 2 * D :] = (
        nn(normed_in, wqkv_ref[:, 2 * D :]) + bias_slice(vec_ref, 2 * D, D)
    ).astype(BF16)

    masks = head_masks()
    lane = lax.broadcasted_iota(jnp.int32, (1, LANES), 1)
    dead = jnp.where(lax.broadcasted_iota(jnp.int32, (1, PAD), 1) < SEQ, 0.0, -1e30)

    def image(b, carry):
        rows = pl.ds(pl.multiple_of(b * PAD, 16), PAD)
        for pair in range(HEADS // 2):
            cols = pair * LANES
            q2 = qkv_ref[rows, cols : cols + LANES]
            k2 = qkv_ref[rows, D + cols : D + cols + LANES]
            v2 = qkv_ref[rows, 2 * D + cols : 2 * D + cols + LANES]
            outs = []
            for mask in masks:
                scores = nt(q2 * mask, k2) * HEAD_DIM ** (-0.5) + dead
                top = jnp.max(scores, axis=-1, keepdims=True)
                grown = jnp.exp(scores - top)
                total = jnp.sum(grown, axis=-1, keepdims=True)
                probs = (grown * (1.0 / total)).astype(BF16)
                outs.append(nn(probs, v2))
            att_ref[rows, cols : cols + LANES] = jnp.where(
                lane < HEAD_DIM, outs[0], outs[1]
            ).astype(BF16)
        return carry

    lax.fori_loop(0, IMGS, image, 0)


def mlp_kernel(swaps, counts_ref, x_ref, up_ref, att_ref, vec_ref, *refs):
    pieces = refs[:8]
    out_ref, gmid_ref, vecg_ref, wout_ref = refs[8:12]
    grads = refs[12:20]
    flat_ref, w1, w2, dw1, dw2, dwo, b1, b1g, pad_ref, go_ref, nm_ref, acc, gacc = refs[20:]
    me = position(swaps)
    count = counts_ref[lax.axis_index(AXES)]
    live = [jnp.where(count > b, 1.0, 0.0).astype(F32) for b in range(IMGS)]
    unpack(me, pieces[:4], flat_ref, 0, 0, SECOND_SPLIT[0])
    unpack(me, pieces[4:], flat_ref, 1, *SECOND_SPLIT)

    def quads(quad, carry):
        rows = pl.ds(pl.multiple_of(quad * 4 * STRIPE, 16), 4 * STRIPE)
        for t in range(FC_TILES):
            w1[t // 3, rows, (t % 3) * LANES : (t % 3 + 1) * LANES] = striped_rows(
                flat_ref, quad, t, FC_TILES
            )
        for t in range(OUT_TILES):
            wout_ref[rows, t * LANES : (t + 1) * LANES] = striped_rows(
                flat_ref, quad, OUT_START + t, OUT_TILES
            )
        return carry

    lax.fori_loop(0, BLOCKS // 4, quads, 0)

    def talls(d, carry):
        rows = pl.ds(pl.multiple_of((d & 7) * TALL, 16), TALL)
        for t in range(OUT_TILES):
            w2[d >> 3, rows, t * LANES : (t + 1) * LANES] = flat_ref[
                d, pl.ds(FC2_START + t, TALL, stride=OUT_TILES), :
            ].astype(BF16)
        return carry

    lax.fori_loop(0, BLOCKS, talls, 0)
    for j in range(CHUNKS):
        b1[j] = bias_slice(vec_ref, 5 * D + j * D, D)

    load_padded(x_ref, pad_ref)
    load_padded(up_ref, acc, live)
    go_ref[...] = acc[...].astype(BF16)
    mid = pad_ref[...] + nn(att_ref[...], wout_ref[...]) + bias_slice(vec_ref, 3 * D, D)
    hat_mid, inv_mid = norm_forward(mid)
    nm_ref[...] = (hat_mid * vec_ref[:, D : 2 * D] + bias_slice(vec_ref, 4 * D, D)).astype(BF16)
    acc[...] = mid + bias_slice(vec_ref, 5 * D + FF, D)
    pad_ref[...] = mid
    gacc[...] = jnp.zeros((ROWS, D), F32)

    def chunk(j, carry):
        hidden = nn(nm_ref[...], w1[j]) + b1[j]
        cdf = 0.5 * (1.0 + lax.erf(hidden * INV_ROOT_TWO))
        act = (hidden * cdf).astype(BF16)
        slope = cdf + hidden * INV_ROOT_TWOPI * jnp.exp(-0.5 * hidden * hidden)
        acc[...] += nn(act, w2[j])
        dw2[j] = tn(act, go_ref[...])
        grad_pre = nt(go_ref[...], w2[j]) * slope
        b1g[j] = jnp.sum(grad_pre, axis=0, keepdims=True)
        grad_pre_bf = grad_pre.astype(BF16)
        dw1[j] = tn(nm_ref[...], grad_pre_bf)
        gacc[...] += nt(grad_pre_bf, w1[j])
        return carry

    lax.fori_loop(0, CHUNKS, chunk, 0)
    for b in range(IMGS):
        out_ref[b] = (acc[b * PAD : b * PAD + SEQ, :] * live[b]).astype(BF16)

    hat_mid, inv_mid = norm_forward(pad_ref[...])
    grad_normed = gacc[...]
    grad_float = go_ref[...].astype(F32)
    grad_mid = grad_float + norm_backward(grad_normed * vec_ref[:, D : 2 * D], hat_mid, inv_mid)
    gmid_ref[...] = grad_mid
    dwo[...] = tn(att_ref[...], grad_mid.astype(BF16))
    vecg_ref[...] = jnp.zeros((1, GAINS + BIASES), F32)
    vecg_ref[:, D : 2 * D] = jnp.sum(grad_normed * hat_mid, axis=0, keepdims=True)
    base = GAINS
    vecg_ref[:, base + 3 * D : base + 4 * D] = jnp.sum(grad_mid, axis=0, keepdims=True)
    vecg_ref[:, base + 4 * D : base + 5 * D] = jnp.sum(grad_normed, axis=0, keepdims=True)
    for j in range(CHUNKS):
        vecg_ref[:, base + (5 + j) * D : base + (6 + j) * D] = b1g[j]
    vecg_ref[:, base + 5 * D + FF :] = jnp.sum(grad_float, axis=0, keepdims=True)

    def pairs(p, carry):
        rows = pl.ds(pl.multiple_of(p * 2 * STRIPE, 8), 2 * STRIPE)
        for t in range(FC_TILES):
            value = dw1[t // 3, rows, (t % 3) * LANES : (t % 3 + 1) * LANES]
            scatter_rows(flat_ref, p, t, FC_TILES, value)
        for t in range(OUT_TILES):
            scatter_rows(
                flat_ref, p, OUT_START + t, OUT_TILES, dwo[rows, t * LANES : (t + 1) * LANES]
            )
        return carry

    lax.fori_loop(0, BLOCKS // 2, pairs, 0)

    def talls_back(d, carry):
        rows = pl.ds(pl.multiple_of((d & 7) * TALL, 16), TALL)
        for t in range(OUT_TILES):
            flat_ref[d, pl.ds(FC2_START + t, TALL, stride=OUT_TILES), :] = dw2[
                d >> 3, rows, t * LANES : (t + 1) * LANES
            ]
        return carry

    lax.fori_loop(0, BLOCKS, talls_back, 0)
    used = FC2_START + FC_ROWS
    flat_ref[:, used:, :] = jnp.zeros((BLOCKS, SECOND_ROWS - used, LANES), F32)
    pack(me, flat_ref, grads[:4], 0, 0, SECOND_SPLIT[0])
    pack(me, flat_ref, grads[4:], 1, *SECOND_SPLIT)


def back_kernel(
    swaps, counts_ref, x_ref, qkv_ref, gmid_ref, wqkv_ref, wout_ref, vec_ref, vecg_ref, *refs
):
    xgrad_ref = refs[0]
    grads = refs[1:5]
    flat_ref, pad_ref, ga_ref, gp_ref, gpb_ref, dwq, vsum = refs[5:]
    me = position(swaps)
    gmid_bf = gmid_ref[...].astype(BF16)
    ga_ref[...] = nt(gmid_bf, wout_ref[...]).astype(BF16)

    masks = head_masks()
    alive = jnp.where(lax.broadcasted_iota(jnp.int32, (PAD, 1), 0) < SEQ, 0.0, -1e30)

    def image(b, carry):
        rows = pl.ds(pl.multiple_of(b * PAD, 16), PAD)
        for pair in range(HEADS // 2):
            cols = pair * LANES
            q2 = qkv_ref[rows, cols : cols + LANES]
            k2 = qkv_ref[rows, D + cols : D + cols + LANES]
            v2 = qkv_ref[rows, 2 * D + cols : 2 * D + cols + LANES]
            g2 = ga_ref[rows, cols : cols + LANES]
            gq = jnp.zeros((PAD, LANES), F32)
            gk = jnp.zeros((PAD, LANES), F32)
            gv = jnp.zeros((PAD, LANES), F32)
            for mask in masks:
                qm = q2 * mask
                gm = g2 * mask
                scores = nt(k2, qm) * HEAD_DIM ** (-0.5) + alive
                top = jnp.max(scores, axis=0, keepdims=True)
                grown = jnp.exp(scores - top)
                total = jnp.sum(grown, axis=0, keepdims=True)
                probs = grown * (1.0 / total)
                grad_probs = nt(v2, gm)
                row_dot = jnp.sum(probs * grad_probs, axis=0, keepdims=True)
                grad_scores = (probs * (grad_probs - row_dot) * HEAD_DIM ** (-0.5)).astype(BF16)
                gv = gv + nn(probs.astype(BF16), gm)
                gk = gk + nn(grad_scores, qm)
                gq = gq + tn(grad_scores, k2 * mask)
            gp_ref[rows, cols : cols + LANES] = gq
            gp_ref[rows, D + cols : D + cols + LANES] = gk
            gp_ref[rows, 2 * D + cols : 2 * D + cols + LANES] = gv
        return carry

    lax.fori_loop(0, IMGS, image, 0)

    load_padded(x_ref, pad_ref)
    hat_in, inv_in = norm_forward(pad_ref[...])
    normed_in = (hat_in * vec_ref[:, :D] + bias_slice(vec_ref, 0, D)).astype(BF16)
    gpb_ref[...] = gp_ref[...].astype(BF16)
    dwq[...] = tn(normed_in, gpb_ref[...])
    grad_in = nt(gpb_ref[...], wqkv_ref[...])
    images_grad = gmid_ref[...] + norm_backward(grad_in * vec_ref[:, :D], hat_in, inv_in)
    pad_ref[...] = images_grad
    for b in range(IMGS):
        xgrad_ref[b] = pad_ref[b * PAD : b * PAD + SEQ, :].astype(BF16)

    vsum[...] = vecg_ref[...]
    vsum[:, :D] = jnp.sum(grad_in * hat_in, axis=0, keepdims=True)
    vsum[:, GAINS : GAINS + D] = jnp.sum(grad_in, axis=0, keepdims=True)
    vsum[:, GAINS + D : GAINS + 2 * D] = jnp.sum(gp_ref[:, :D], axis=0, keepdims=True)
    vsum[:, GAINS + 2 * D : GAINS + 3 * D] = jnp.sum(gp_ref[:, 2 * D :], axis=0, keepdims=True)

    flat_ref[:, BIAS_ROW:, :] = jnp.zeros((BLOCKS, FIRST_ROWS - BIAS_ROW, LANES), F32)
    flat_ref[:, BIAS_ROW, :] = collect(vsum[:, GAINS:], BIAS_PART, BIASES)
    flat_ref[:, GAIN_ROW, :] = collect(vsum[:, :GAINS], GAIN_PART, GAINS)

    def pairs(p, carry):
        rows = pl.ds(pl.multiple_of(p * 2 * STRIPE, 8), 2 * STRIPE)
        for t in range(QKV_TILES):
            scatter_rows(flat_ref, p, t, QKV_TILES, dwq[rows, t * LANES : (t + 1) * LANES])
        return carry

    lax.fori_loop(0, BLOCKS // 2, pairs, 0)
    pack(me, flat_ref, grads, 0, 0, FIRST_ROWS)


def shape(dims, kind):
    return jax.ShapeDtypeStruct(dims, kind)


def call(kernel, swaps, outs, scratch, cost, *operands):
    specs = [pl.BlockSpec(memory_space=pltpu.SMEM)]
    specs += [pl.BlockSpec(memory_space=pltpu.VMEM)] * (len(operands) - 1)
    return pl.pallas_call(
        functools.partial(kernel, swaps),
        out_shape=outs,
        in_specs=specs,
        out_specs=[pl.BlockSpec(memory_space=pltpu.VMEM)] * len(outs),
        scratch_shapes=scratch,
        compiler_params=pltpu.CompilerParams(vmem_limit_bytes=56 * 1024 * 1024),
        cost_estimate=pl.CostEstimate(flops=cost, transcendentals=0, bytes_accessed=4_000_000),
    )(*operands)


def attend(swaps, counts, images, pieces):
    outs = [
        shape((D, 3 * D), BF16),
        shape((1, GAINS + BIASES), F32),
        shape((ROWS, 3 * D), BF16),
        shape((ROWS, D), BF16),
    ]
    scratch = [
        pltpu.VMEM((BLOCKS, FIRST_ROWS, LANES), F32),
        pltpu.VMEM((ROWS, D), F32),
    ]
    return call(attend_kernel, swaps, outs, scratch, 5_000_000_000, counts, images, *pieces)


def piece_shapes(*split):
    return [shape((8, rows, LANES), BF16) for rows in split for _ in range(4)]


def mlp(swaps, counts, images, upstream, attended, vec, pieces):
    outs = [
        shape((IMGS, SEQ, D), BF16),
        shape((ROWS, D), F32),
        shape((1, GAINS + BIASES), F32),
        shape((D, D), BF16),
    ] + piece_shapes(*SECOND_SPLIT)
    scratch = [
        pltpu.VMEM((BLOCKS, SECOND_ROWS, LANES), F32),
        pltpu.VMEM((CHUNKS, D, D), BF16),
        pltpu.VMEM((CHUNKS, D, D), BF16),
        pltpu.VMEM((CHUNKS, D, D), F32),
        pltpu.VMEM((CHUNKS, D, D), F32),
        pltpu.VMEM((D, D), F32),
        pltpu.VMEM((CHUNKS, 1, D), F32),
        pltpu.VMEM((CHUNKS, 1, D), F32),
        pltpu.VMEM((ROWS, D), F32),
        pltpu.VMEM((ROWS, D), BF16),
        pltpu.VMEM((ROWS, D), BF16),
        pltpu.VMEM((ROWS, D), F32),
        pltpu.VMEM((ROWS, D), F32),
    ]
    return call(
        mlp_kernel, swaps, outs, scratch, 8_000_000_000,
        counts, images, upstream, attended, vec, *pieces,
    )


def back(swaps, counts, images, qkv, grad_mid, w_qkv, w_out, vec, vec_grad):
    outs = [shape((IMGS, SEQ, D), BF16)] + piece_shapes(FIRST_ROWS)
    scratch = [
        pltpu.VMEM((BLOCKS, FIRST_ROWS, LANES), F32),
        pltpu.VMEM((ROWS, D), F32),
        pltpu.VMEM((ROWS, D), BF16),
        pltpu.VMEM((ROWS, 3 * D), F32),
        pltpu.VMEM((ROWS, 3 * D), BF16),
        pltpu.VMEM((D, 3 * D), F32),
        pltpu.VMEM((1, GAINS + BIASES), F32),
    ]
    return call(
        back_kernel, swaps, outs, scratch, 6_000_000_000,
        counts, images, qkv, grad_mid, w_qkv, w_out, vec, vec_grad,
    )


def exchange(value, mask):
    return lax.ppermute(value, AXES, [(i, i ^ mask) for i in range(BLOCKS)])


def gather_line(block):
    held = block[None]
    for mask in (Z_LOW, Z_HIGH, Y_BIT):
        held = jnp.concatenate([held, exchange(held, mask)])
    other = exchange(held, X_BIT)
    core = exchange(held, CORE_BIT)
    last = exchange(other, CORE_BIT)
    return [held, other, core, last]


def reduce_line(pieces):
    keep, keep_far, send, send_far = pieces
    from_core = exchange(send_far, CORE_BIT)
    far_sum = keep_far.astype(F32) + from_core.astype(F32)
    crossed = exchange(far_sum.astype(BF16), X_BIT)
    from_core = exchange(send, CORE_BIT)
    held = keep.astype(F32) + from_core.astype(F32) + crossed.astype(F32)
    for mask in (Y_BIT, Z_HIGH, Z_LOW):
        half = held.shape[0] // 2
        crossed = exchange(held[half:].astype(BF16), mask)
        held = held[:half] + crossed.astype(F32)
    return held[0]


def gather_blocks(block, split):
    line = [block]
    for mask in (Z_LOW, Z_HIGH, Z_LOW + Z_HIGH):
        line.append(exchange(block, mask))
    colors = []
    for color, (near, far) in enumerate(((Y_BIT, X_BIT), (X_BIT, Y_BIT))):
        part = slice(0, split[0]) if color == 0 else slice(split[0], None)
        first = jnp.stack([piece[part] for piece in line])
        colors.append((first, exchange(first, near), far))
    pieces = []
    for first, second, far in colors:
        plane = jnp.concatenate([first, second])
        other = exchange(plane, far)
        core = exchange(plane, CORE_BIT)
        last = exchange(other, CORE_BIT)
        pieces += [plane, other, core, last]
    return pieces


def reduce_blocks(pieces):
    done = []
    for color, (near, far) in enumerate(((Y_BIT, X_BIT), (X_BIT, Y_BIT))):
        keep, keep_far, send, send_far = pieces[4 * color : 4 * color + 4]
        from_core = exchange(send_far, CORE_BIT)
        far_sum = keep_far.astype(F32) + from_core.astype(F32)
        crossed = exchange(far_sum.astype(BF16), far)
        from_core = exchange(send, CORE_BIT)
        plane = keep.astype(F32) + from_core.astype(F32) + crossed.astype(F32)
        crossed = exchange(plane[4:].astype(BF16), near)
        done.append(plane[:4] + crossed.astype(F32))
    line = jnp.concatenate(done, axis=1)
    total = line[0]
    for step, mask in ((1, Z_LOW), (2, Z_HIGH), (3, Z_LOW + Z_HIGH)):
        crossed = exchange(line[step].astype(BF16), mask)
        total = total + crossed.astype(F32)
    return total


def ordered_pieces(whole, split):
    cube = whole.reshape(2, 2, 4, 2, -1, LANES)
    if len(split) == 1:
        pieces = [cube[x, core].swapaxes(0, 1) for core in range(2) for x in range(2)]
        return [piece.reshape((8,) + piece.shape[2:]) for piece in pieces]
    near, far = cube[..., : split[0], :], cube[..., split[0] :, :]
    pieces = [near[x, core].swapaxes(0, 1) for core in range(2) for x in range(2)]
    pieces += [far[:, core, :, y] for core in range(2) for y in range(2)]
    return [piece.reshape((8,) + piece.shape[2:]) for piece in pieces]


def blocks_of_pieces(pieces):
    first = jnp.stack(pieces[:4]).reshape(2, 2, 2, 4, -1, LANES)
    if len(pieces) == 4:
        return first.transpose(1, 0, 3, 2, 4, 5).reshape(BLOCKS, -1, LANES)
    second = jnp.stack(pieces[4:]).reshape(2, 2, 2, 4, -1, LANES)
    first = first.transpose(1, 0, 3, 2, 4, 5)
    second = second.transpose(2, 0, 3, 1, 4, 5)
    return jnp.concatenate([first, second], axis=4).reshape(BLOCKS, -1, LANES)


def block_rows(flat, rows):
    flat = flat.reshape(flat.shape[:-1] + (-1,))
    short = rows * LANES - flat.shape[-1]
    if short:
        flat = jnp.pad(flat, [(0, 0)] * (flat.ndim - 1) + [(0, short)])
    return flat.reshape(flat.shape[:-1] + (rows, LANES))


def padded_rows(parts, rows):
    short = rows - sum(part.shape[-2] for part in parts)
    filler = jnp.zeros(parts[0].shape[:-2] + (short, LANES), parts[0].dtype)
    return jnp.concatenate([*parts, filler], axis=-2)


def build_first(qkv, gains, biases):
    parts = [block_rows(qkv, QKV_ROWS), block_rows(biases, 1), block_rows(gains, 1)]
    return padded_rows(parts, FIRST_ROWS)


def build_second(out, fc1, fc2):
    parts = [block_rows(fc1, FC_ROWS), block_rows(out, OUT_ROWS), block_rows(fc2, FC_ROWS)]
    return padded_rows(parts, SECOND_ROWS)


def flat_rows(block, start, rows):
    return block[..., start : start + rows, :].reshape(block.shape[:-2] + (-1,))


def split_blocks(first, second):
    return (
        flat_rows(first, 0, QKV_ROWS),
        flat_rows(second, OUT_START, OUT_ROWS),
        flat_rows(second, 0, FC_ROWS),
        flat_rows(second, FC2_START, FC_ROWS),
        first[..., GAIN_ROW, :GAIN_PART],
        first[..., BIAS_ROW, :BIAS_PART],
    )


def adam_update(weight, gradient, moment_one, moment_two, step_rate, decayed):
    first_new = BETA_ONE * moment_one + (1.0 - BETA_ONE) * gradient
    second_new = BETA_TWO * moment_two + (1.0 - BETA_TWO) * gradient * gradient
    first_hat = first_new / (1.0 - BETA_ONE**ADAM_STEP)
    second_hat = second_new / (1.0 - BETA_TWO**ADAM_STEP)
    change = first_hat / (jnp.sqrt(second_hat) + ADAM_EPS)
    if decayed:
        change = change + DECAY_RATE * weight
    return (weight - step_rate * change, first_new, second_new)


def device_step(devices, images, counts, upstream, *state):
    masters, firsts, seconds = state[:6], state[6:12], state[12:18]
    lowered = [master.astype(BF16) for master in masters]
    swaps = devices == BLOCKS
    if swaps:
        qkv, out, fc1, fc2, gains, biases = lowered
        first = gather_line(build_first(qkv, gains, biases))
        second = gather_blocks(build_second(out, fc1, fc2), SECOND_SPLIT)
    else:
        qkv, out, fc1, fc2, gains, biases = [
            lax.all_gather(part, AXES, axis=0, tiled=True).reshape(BLOCKS, -1) for part in lowered
        ]
        first = ordered_pieces(build_first(qkv, gains, biases), (FIRST_ROWS,))
        second = ordered_pieces(build_second(out, fc1, fc2), SECOND_SPLIT)
    w_qkv, vec, qkv, attended = attend(swaps, counts, images, first)
    block_out, grad_mid, vec_grad, w_out, *second_grads = mlp(
        swaps, counts, images, upstream, attended, vec, second
    )
    images_grad, *first_grads = back(
        swaps, counts, images, qkv, grad_mid, w_qkv, w_out, vec, vec_grad
    )
    if swaps:
        second_sum = reduce_blocks(second_grads)
        first_sum = reduce_line(first_grads)
        owned = split_blocks(first_sum, second_sum)
    else:
        owned = tuple(
            lax.psum_scatter(part.reshape(-1), AXES, scatter_dimension=0, tiled=True)
            for part in split_blocks(
                blocks_of_pieces(first_grads).astype(F32),
                blocks_of_pieces(second_grads).astype(F32),
            )
        )
    updates = [
        adam_update(masters[p], owned[p], firsts[p], seconds[p], RATES[p], DECAYED[p])
        for p in range(6)
    ]
    return (
        block_out,
        images_grad,
        *owned,
        *(update[0] for update in updates),
        *(update[1] for update in updates),
        *(update[2] for update in updates),
    )


def solution(mesh):
    devices = math.prod(mesh.shape.values())
    slots = P(AXES, None, None)
    flat = P(AXES)

    def step(*args):
        return device_step(devices, *args)

    return jax.shard_map(
        step,
        mesh=mesh,
        in_specs=(slots, P(), slots) + (flat,) * 18,
        out_specs=(slots, slots) + (flat,) * 24,
        check_vma=False,
    )
```

profile of v0, /device:TPU:0, one launch (start us, length us, event | category | flops | bytes accessed | tf_op | source)
XLA Modules:
  0.0 116.8 jit_solution(17766728887744350897)
XLA Ops:
  2.4 5.1 %collective-permute-start.8 = (bf16[336,128]{1,0:T(8,128)(2,1)S(1)}, bf16[336,128]{1,0:T(8,128)(2,1)S(1)}, u32[]{:S(2)}, u32[]{:S(2)}) collective-permute-start(bf16[336,128]{1,0:T(8,128)(2,1)S(1)} %pad_maximum_fusion.5), channel_id=1, source_target_pairs={{0,6},{1,7},{2,4},{3,5},{4,2},{5,3},{6,0},{7,1},{8,14},{9,15},{10,... | collective-permute-start | bytes 258056 | tf_op jit(solution)/shard_map/ppermute | solution.py:498
  9.9 3.8 %collective-permute-done = bf16[1,112,128]{2,1,0:T(8,128)(2,1)S(1)} collective-permute-done((bf16[1,112,128]{2,1,0:T(8,128)(2,1)S(1)}, bf16[1,112,128]{2,1,0:T(8,128)(2,1)S(1)}, u32[]{:S(2)}, u32[]{:S(2)}) %collective-permute-start) | collective-permute-done | bytes 28704 | tf_op jit(solution)/shard_map/ppermute | solution.py:498
  13.7 1.6 %collective-permute-start.1 = (bf16[2,112,128]{2,1,0:T(8,128)(2,1)S(1)}, bf16[2,112,128]{2,1,0:T(8,128)(2,1)S(1)}, u32[]{:S(2)}, u32[]{:S(2)}) collective-permute-start(bf16[2,112,128]{2,1,0:T(8,128)(2,1)S(1)} %pad_maximum_fusion.6), channel_id=1, source_target_pairs={{0,4},{1,5},{2,6},{3,7},{4,0},{5,1},{6,2},{7,3},{8,12},{9,13},{10,... | collective-permute-start | bytes 172040 | tf_op jit(solution)/shard_map/ppermute | solution.py:498
  15.3 4.0 %collective-permute-done.1 = bf16[2,112,128]{2,1,0:T(8,128)(2,1)S(1)} collective-permute-done((bf16[2,112,128]{2,1,0:T(8,128)(2,1)S(1)}, bf16[2,112,128]{2,1,0:T(8,128)(2,1)S(1)}, u32[]{:S(2)}, u32[]{:S(2)}) %collective-permute-start.1) | collective-permute-done | bytes 57376 | tf_op jit(solution)/shard_map/ppermute | solution.py:498
  19.4 1.6 %collective-permute-start.2 = (bf16[4,112,128]{2,1,0:T(8,128)(2,1)S(1)}, bf16[4,112,128]{2,1,0:T(8,128)(2,1)S(1)}, u32[]{:S(2)}, u32[]{:S(2)}) collective-permute-start(bf16[4,112,128]{2,1,0:T(8,128)(2,1)S(1)} %pad_maximum_fusion.4), channel_id=1, source_target_pairs={{0,1},{1,0},{2,3},{3,2},{4,5},{5,4},{6,7},{7,6},{8,9},{9,8},{10,11... | collective-permute-start | bytes 344072 | tf_op jit(solution)/shard_map/ppermute | solution.py:498
  21.7 1.6 %collective-permute-start.13 = (bf16[4,176,128]{2,1,0:T(8,128)(2,1)S(1)}, bf16[4,176,128]{2,1,0:T(8,128)(2,1)S(1)}, u32[]{:S(2)}, u32[]{:S(2)}) collective-permute-start(bf16[4,176,128]{2,1,0:T(8,128)(2,1)S(1)} %pad_maximum_fusion.2), channel_id=1, source_target_pairs={{0,16},{1,17},{2,18},{3,19},{4,20},{5,21},{6,22},{7,23},{8,24},{9,... | collective-permute-start | bytes 540680 | tf_op jit(solution)/shard_map/ppermute | solution.py:498
  24.3 1.6 %collective-permute-start.3 = (bf16[8,112,128]{2,1,0:T(8,128)(2,1)S(1)}, bf16[8,112,128]{2,1,0:T(8,128)(2,1)S(1)}, u32[]{:S(2)}, u32[]{:S(2)}) collective-permute-start(bf16[8,112,128]{2,1,0:T(8,128)(2,1)S(1)} %pad_maximum_fusion.1.refs_0_), channel_id=1, source_target_pairs={{0,16},{1,17},{2,18},{3,19},{4,20},{5,21},{6,22},{7,23},{8,24},{9,... | collective-permute-start | bytes 688136 | tf_op jit(solution)/shard_map/ppermute | solution.py:498
  25.9 2.2 %collective-permute-done.13 = bf16[4,176,128]{2,1,0:T(8,128)(2,1)S(1)} collective-permute-done((bf16[4,176,128]{2,1,0:T(8,128)(2,1)S(1)}, bf16[4,176,128]{2,1,0:T(8,128)(2,1)S(1)}, u32[]{:S(2)}, u32[]{:S(2)}) %collective-permute-start.13) | collective-permute-done | bytes 180256 | tf_op jit(solution)/shard_map/ppermute | solution.py:498
  28.1 2.6 %collective-permute-start.14 = (bf16[8,176,128]{2,1,0:T(8,128)(2,1)S(1)}, bf16[8,176,128]{2,1,0:T(8,128)(2,1)S(1)}, u32[]{:S(2)}, u32[]{:S(2)}) collective-permute-start(bf16[8,176,128]{2,1,0:T(8,128)(2,1)S(1)} %constant_dynamic-update-slice_fusion.5.refs_4_), channel_id=1, source_target_pairs={{0,1},{1,0},{2,3},{3,2},{4,5},{5,4},{6,7},{7,6},{8,9},{9,8},{10,11... | collective-permute-start | bytes 1081352 | tf_op jit(solution)/shard_map/ppermute | solution.py:498
  30.8 1.6 %collective-permute-start.10 = (bf16[8,160,128]{2,1,0:T(8,128)(2,1)S(1)}, bf16[8,160,128]{2,1,0:T(8,128)(2,1)S(1)}, u32[]{:S(2)}, u32[]{:S(2)}) collective-permute-start(bf16[8,160,128]{2,1,0:T(8,128)(2,1)S(1)} %constant_dynamic-update-slice_fusion.refs_0_), channel_id=1, source_target_pairs={{0,16},{1,17},{2,18},{3,19},{4,20},{5,21},{6,22},{7,23},{8,24},{9,... | collective-permute-start | bytes 983048 | tf_op jit(solution)/shard_map/ppermute | solution.py:498
  35.2 2.8 %collective-permute-done.10.refs_1_ = bf16[8,160,128]{2,1,0:T(8,128)(2,1)S(1)} collective-permute-done((bf16[8,160,128]{2,1,0:T(8,128)(2,1)S(1)}, bf16[8,160,128]{2,1,0:T(8,128)(2,1)S(1)}, u32[]{:S(2)}, u32[]{:S(2)}) %collective-permute-start.10) | collective-permute-done | bytes 327712 | tf_op jit(solution)/shard_map/ppermute | solution.py:498
  39.1 6.3 %shard_map.404 = (bf16[384,1152]{1,0:T(8,128)(2,1)}, f32[1,4608]{1,0:T(1,128)}, bf16[416,1152]{1,0:T(8,128)(2,1)}, bf16[416,384]{1,0:T(8,128)(2,1)}) custom-call(s32[32]{0:T(128)} %counts_ref.5, bf16[2,197,384]{2,1,0:T(8,128)(2,1)} %copy.48.x_ref, bf16[8,112,128]{2,1,0:T(8,128)(2,1)} %copy-done.10, bf16[8,112,128]{2,1,0:T(8,128)(2,1)} %copy-done.40, ...), custom_call_target="tpu_custom_call" | custom-call | flops 5000000000 | bytes 4000000 | tf_op jit(solution)/shard_map/pallas_call | solution.py:423
  46.5 15.0 %shard_map.405 = (bf16[2,197,384]{2,1,0:T(8,128)(2,1)}, f32[416,384]{1,0:T(8,128)}, f32[1,4608]{1,0:T(1,128)}, bf16[384,384]{1,0:T(8,128)(2,1)}, bf16[8,160,128]...) custom-call(s32[32]{0:T(128)} %counts_ref.5, ...), custom_call_target="tpu_custom_call" | custom-call | flops 8000000000 | bytes 4000000 | tf_op jit(solution)/shard_map/pallas_call | solution.py:423
  61.6 10.0 %shard_map.406 = (bf16[2,197,384]{2,1,0:T(8,128)(2,1)}, bf16[8,112,128]{2,1,0:T(8,128)(2,1)}, bf16[8,112,128]{2,1,0:T(8,128)(2,1)}, bf16[8,112,128]{2,1,0:T(8,128)(2,1)}, bf16[8,112,128]{2,1,0:T(8,128)(2,1)}) custom-call(s32[32]{0:T(128)} %counts_ref.5, bf16[2,197,384]{2,1,0:T(8,128)(2,1)} %copy.48.x_ref, bf16[416,1152]{1,0:T(8,128)(2,1)} %get-tuple-element.50.qkv_ref, ...), custom_call_target="tpu_custom_call" | custom-call | flops 6000000000 | bytes 4000000 | tf_op jit(solution)/shard_map/pallas_call | solution.py:423
  74.3 1.6 %collective-permute-start.19 = (bf16[8,112,128]{2,1,0:T(8,128)(2,1)S(1)}, bf16[8,112,128]{2,1,0:T(8,128)(2,1)S(1)}, u32[]{:S(2)}, u32[]{:S(2)}) collective-permute-start(bf16[8,112,128]{2,1,0:T(8,128)(2,1)S(1)} %add_convert_fusion.2), channel_id=1, source_target_pairs={{0,16},{1,17},{2,18},{3,19},{4,20},{5,21},{6,22},{7,23},{8,24},{9,... | collective-permute-start | bytes 688136 | tf_op jit(solution)/shard_map/ppermute | solution.py:498
  78.8 3.2 %collective-permute-done.19 = bf16[8,112,128]{2,1,0:T(8,128)(2,1)S(1)} collective-permute-done((bf16[8,112,128]{2,1,0:T(8,128)(2,1)S(1)}, bf16[8,112,128]{2,1,0:T(8,128)(2,1)S(1)}, u32[]{:S(2)}, u32[]{:S(2)}) %collective-permute-start.19) | collective-permute-done | bytes 229408 | tf_op jit(solution)/shard_map/ppermute | solution.py:498
  83.1 1.6 %collective-permute-start.25 = (bf16[8,160,128]{2,1,0:T(8,128)(2,1)S(1)}, bf16[8,160,128]{2,1,0:T(8,128)(2,1)S(1)}, u32[]{:S(2)}, u32[]{:S(2)}) collective-permute-start(bf16[8,160,128]{2,1,0:T(8,128)(2,1)S(1)} %add_convert_fusion.1), channel_id=1, source_target_pairs={{0,16},{1,17},{2,18},{3,19},{4,20},{5,21},{6,22},{7,23},{8,24},{9,... | collective-permute-start | bytes 983048 | tf_op jit(solution)/shard_map/ppermute | solution.py:498
  84.7 2.3 %collective-permute-done.20 = bf16[4,112,128]{2,1,0:T(8,128)(2,1)S(1)} collective-permute-done((bf16[4,112,128]{2,1,0:T(8,128)(2,1)S(1)}, bf16[4,112,128]{2,1,0:T(8,128)(2,1)S(1)}, u32[]{:S(2)}, u32[]{:S(2)}) %collective-permute-start.20) | collective-permute-done | bytes 114720 | tf_op jit(solution)/shard_map/ppermute | solution.py:498
  89.3 2.9 %collective-permute-done.21 = bf16[2,112,128]{2,1,0:T(8,128)(2,1)S(1)} collective-permute-done((bf16[2,112,128]{2,1,0:T(8,128)(2,1)S(1)}, bf16[2,112,128]{2,1,0:T(8,128)(2,1)S(1)}, u32[]{:S(2)}, u32[]{:S(2)}) %collective-permute-start.21) | collective-permute-done | bytes 57376 | tf_op jit(solution)/shard_map/ppermute | solution.py:498
  92.2 2.3 %collective-permute-start.22 = (bf16[1,112,128]{2,1,0:T(8,128)(2,1)S(1)}, bf16[1,112,128]{2,1,0:T(8,128)(2,1)S(1)}, u32[]{:S(2)}, u32[]{:S(2)}) collective-permute-start(bf16[1,112,128]{2,1,0:T(8,128)(2,1)S(1)} %slice.205), channel_id=1, source_target_pairs={{0,2},{1,3},{2,0},{3,1},{4,6},{5,7},{6,4},{7,5},{8,10},{9,11},{10,... | collective-permute-start | bytes 86024 | tf_op jit(solution)/shard_map/ppermute | solution.py:498
  98.5 1.6 %collective-permute-start.30 = (bf16[4,176,128]{2,1,0:T(8,128)(2,1)S(1)}, bf16[4,176,128]{2,1,0:T(8,128)(2,1)S(1)}, u32[]{:S(2)}, u32[]{:S(2)}) collective-permute-start(bf16[4,176,128]{2,1,0:T(8,128)(2,1)S(1)} %slice.201), channel_id=1, source_target_pairs={{0,16},{1,17},{2,18},{3,19},{4,20},{5,21},{6,22},{7,23},{8,24},{9,... | collective-permute-start | bytes 540680 | tf_op jit(solution)/shard_map/ppermute | solution.py:498
  100.2 3.9 %collective-permute-done.30 = bf16[4,176,128]{2,1,0:T(8,128)(2,1)S(1)} collective-permute-done((bf16[4,176,128]{2,1,0:T(8,128)(2,1)S(1)}, bf16[4,176,128]{2,1,0:T(8,128)(2,1)S(1)}, u32[]{:S(2)}, u32[]{:S(2)}) %collective-permute-start.30) | collective-permute-done | bytes 180256 | tf_op jit(solution)/shard_map/ppermute | solution.py:498
  104.2 2.9 %collective-permute-start.31 = (bf16[336,128]{1,0:T(8,128)(2,1)S(1)}, bf16[336,128]{1,0:T(8,128)(2,1)S(1)}, u32[]{:S(2)}, u32[]{:S(2)}) collective-permute-start(bf16[336,128]{1,0:T(8,128)(2,1)S(1)} %get-tuple-element.122), channel_id=1, source_target_pairs={{0,2},{1,3},{2,0},{3,1},{4,6},{5,7},{6,4},{7,5},{8,10},{9,11},{10,... | collective-permute-start | bytes 258056 | tf_op jit(solution)/shard_map/ppermute | solution.py:498
  109.5 3.9 %collective-permute-done.33 = bf16[336,128]{1,0:T(8,128)(2,1)S(1)} collective-permute-done((bf16[336,128]{1,0:T(8,128)(2,1)S(1)}, bf16[336,128]{1,0:T(8,128)(2,1)S(1)}, u32[]{:S(2)}, u32[]{:S(2)}) %collective-permute-start.33) | collective-permute-done | bytes 86048 | tf_op jit(solution)/shard_map/ppermute | solution.py:498
  (193 shorter events, 29.7 us)
Async XLA Ops:
  2.4 18.6 %collective-permute-start.8 = (bf16[336,128]{1,0:T(8,128)(2,1)S(1)}, bf16[336,128]{1,0:T(8,128)(2,1)S(1)}, u32[]{:S(2)}, u32[]{:S(2)}) collective-permute-start(bf16[336,128]{1,0:T(8,128)(2,1)S(1)} %pad_maximum_fusion.5), channel_id=1, source_target_pairs={{0,6},{1,7},{2,4},{3,5},{4,2},{5,3},{6,0},{7,1},{8,14},{9,15},{10,... | collective-permute-start | bytes 258056 | tf_op jit(solution)/shard_map/ppermute | solution.py:498
  7.6 13.4 %collective-permute-start.7 = (bf16[336,128]{1,0:T(8,128)(2,1)S(1)}, bf16[336,128]{1,0:T(8,128)(2,1)S(1)}, u32[]{:S(2)}, u32[]{:S(2)}) collective-permute-start(bf16[336,128]{1,0:T(8,128)(2,1)S(1)} %pad_maximum_fusion.5), channel_id=1, source_target_pairs={{0,4},{1,5},{2,6},{3,7},{4,0},{5,1},{6,2},{7,3},{8,12},{9,13},{10,... | collective-permute-start | bytes 258056 | tf_op jit(solution)/shard_map/ppermute | solution.py:498
  7.6 13.5 %collective-permute-start.6 = (bf16[336,128]{1,0:T(8,128)(2,1)S(1)}, bf16[336,128]{1,0:T(8,128)(2,1)S(1)}, u32[]{:S(2)}, u32[]{:S(2)}) collective-permute-start(bf16[336,128]{1,0:T(8,128)(2,1)S(1)} %pad_maximum_fusion.5), channel_id=1, source_target_pairs={{0,2},{1,3},{2,0},{3,1},{4,6},{5,7},{6,4},{7,5},{8,10},{9,11},{10,... | collective-permute-start | bytes 258056 | tf_op jit(solution)/shard_map/ppermute | solution.py:498
  13.7 5.7 %collective-permute-start.1 = (bf16[2,112,128]{2,1,0:T(8,128)(2,1)S(1)}, bf16[2,112,128]{2,1,0:T(8,128)(2,1)S(1)}, u32[]{:S(2)}, u32[]{:S(2)}) collective-permute-start(bf16[2,112,128]{2,1,0:T(8,128)(2,1)S(1)} %pad_maximum_fusion.6), channel_id=1, source_target_pairs={{0,4},{1,5},{2,6},{3,7},{4,0},{5,1},{6,2},{7,3},{8,12},{9,13},{10,... | collective-permute-start | bytes 172040 | tf_op jit(solution)/shard_map/ppermute | solution.py:498
  21.1 9.6 %collective-permute-start.9 = (bf16[4,160,128]{2,1,0:T(8,128)(2,1)S(1)}, bf16[4,160,128]{2,1,0:T(8,128)(2,1)S(1)}, u32[]{:S(2)}, u32[]{:S(2)}) collective-permute-start(bf16[4,160,128]{2,1,0:T(8,128)(2,1)S(1)} %pad_maximum_fusion.3), channel_id=1, source_target_pairs={{0,1},{1,0},{2,3},{3,2},{4,5},{5,4},{6,7},{7,6},{8,9},{9,8},{10,11... | collective-permute-start | bytes 491528 | tf_op jit(solution)/shard_map/ppermute | solution.py:498
  21.7 6.4 %collective-permute-start.13 = (bf16[4,176,128]{2,1,0:T(8,128)(2,1)S(1)}, bf16[4,176,128]{2,1,0:T(8,128)(2,1)S(1)}, u32[]{:S(2)}, u32[]{:S(2)}) collective-permute-start(bf16[4,176,128]{2,1,0:T(8,128)(2,1)S(1)} %pad_maximum_fusion.2), channel_id=1, source_target_pairs={{0,16},{1,17},{2,18},{3,19},{4,20},{5,21},{6,22},{7,23},{8,24},{9,... | collective-permute-start | bytes 540680 | tf_op jit(solution)/shard_map/ppermute | solution.py:498
  24.3 8.7 %collective-permute-start.3 = (bf16[8,112,128]{2,1,0:T(8,128)(2,1)S(1)}, bf16[8,112,128]{2,1,0:T(8,128)(2,1)S(1)}, u32[]{:S(2)}, u32[]{:S(2)}) collective-permute-start(bf16[8,112,128]{2,1,0:T(8,128)(2,1)S(1)} %pad_maximum_fusion.1.refs_0_), channel_id=1, source_target_pairs={{0,16},{1,17},{2,18},{3,19},{4,20},{5,21},{6,22},{7,23},{8,24},{9,... | collective-permute-start | bytes 688136 | tf_op jit(solution)/shard_map/ppermute | solution.py:498
  28.1 9.8 %collective-permute-start.14 = (bf16[8,176,128]{2,1,0:T(8,128)(2,1)S(1)}, bf16[8,176,128]{2,1,0:T(8,128)(2,1)S(1)}, u32[]{:S(2)}, u32[]{:S(2)}) collective-permute-start(bf16[8,176,128]{2,1,0:T(8,128)(2,1)S(1)} %constant_dynamic-update-slice_fusion.5.refs_4_), channel_id=1, source_target_pairs={{0,1},{1,0},{2,3},{3,2},{4,5},{5,4},{6,7},{7,6},{8,9},{9,8},{10,11... | collective-permute-start | bytes 1081352 | tf_op jit(solution)/shard_map/ppermute | solution.py:498
  30.8 7.1 %collective-permute-start.10 = (bf16[8,160,128]{2,1,0:T(8,128)(2,1)S(1)}, bf16[8,160,128]{2,1,0:T(8,128)(2,1)S(1)}, u32[]{:S(2)}, u32[]{:S(2)}) collective-permute-start(bf16[8,160,128]{2,1,0:T(8,128)(2,1)S(1)} %constant_dynamic-update-slice_fusion.refs_0_), channel_id=1, source_target_pairs={{0,16},{1,17},{2,18},{3,19},{4,20},{5,21},{6,22},{7,23},{8,24},{9,... | collective-permute-start | bytes 983048 | tf_op jit(solution)/shard_map/ppermute | solution.py:498
  34.6 10.9 %collective-permute-start.11 = (bf16[8,160,128]{2,1,0:T(8,128)(2,1)S(1)}, bf16[8,160,128]{2,1,0:T(8,128)(2,1)S(1)}, u32[]{:S(2)}, u32[]{:S(2)}) collective-permute-start(bf16[8,160,128]{2,1,0:T(8,128)(2,1)S(1)} %constant_dynamic-update-slice_fusion.refs_0_), channel_id=1, source_target_pairs={{0,8},{1,9},{2,10},{3,11},{4,12},{5,13},{6,14},{7,15},{8,0},{9,1},... | collective-permute-start | bytes 983048 | tf_op jit(solution)/shard_map/ppermute | solution.py:498
  35.1 10.4 %collective-permute-start.15 = (bf16[8,176,128]{2,1,0:T(8,128)(2,1)S(1)}, bf16[8,176,128]{2,1,0:T(8,128)(2,1)S(1)}, u32[]{:S(2)}, u32[]{:S(2)}) collective-permute-start(bf16[8,176,128]{2,1,0:T(8,128)(2,1)S(1)} %constant_dynamic-update-slice_fusion.5.refs_4_), channel_id=1, source_target_pairs={{0,8},{1,9},{2,10},{3,11},{4,12},{5,13},{6,14},{7,15},{8,0},{9,1},... | collective-permute-start | bytes 1081352 | tf_op jit(solution)/shard_map/ppermute | solution.py:498
  37.9 7.6 %collective-permute-start.12 = (bf16[8,160,128]{2,1,0:T(8,128)(2,1)S(1)}, bf16[8,160,128]{2,1,0:T(8,128)(2,1)S(1)}, u32[]{:S(2)}, u32[]{:S(2)}) collective-permute-start(bf16[8,160,128]{2,1,0:T(8,128)(2,1)S(1)} %collective-permute-done.10.refs_1_), channel_id=1, source_target_pairs={{0,8},{1,9},{2,10},{3,11},{4,12},{5,13},{6,14},{7,15},{8,0},{9,1},... | collective-permute-start | bytes 983048 | tf_op jit(solution)/shard_map/ppermute | solution.py:498
  37.9 7.6 %collective-permute-start.16 = (bf16[8,176,128]{2,1,0:T(8,128)(2,1)S(1)}, bf16[8,176,128]{2,1,0:T(8,128)(2,1)S(1)}, u32[]{:S(2)}, u32[]{:S(2)}) collective-permute-start(bf16[8,176,128]{2,1,0:T(8,128)(2,1)S(1)} %collective-permute-done.14.refs_5_), channel_id=1, source_target_pairs={{0,8},{1,9},{2,10},{3,11},{4,12},{5,13},{6,14},{7,15},{8,0},{9,1},... | collective-permute-start | bytes 1081352 | tf_op jit(solution)/shard_map/ppermute | solution.py:498
  71.7 6.7 %collective-permute-start.17 = (bf16[8,112,128]{2,1,0:T(8,128)(2,1)}, bf16[8,112,128]{2,1,0:T(8,128)(2,1)S(1)}, u32[]{:S(2)}, u32[]{:S(2)}) collective-permute-start(bf16[8,112,128]{2,1,0:T(8,128)(2,1)} %get-tuple-element.57), channel_id=1, source_target_pairs={{0,8},{1,9},{2,10},{3,11},{4,12},{5,13},{6,14},{7,15},{8,0},{9,1},... | collective-permute-start | bytes 688136 | tf_op jit(solution)/shard_map/ppermute | solution.py:498
  74.3 7.7 %collective-permute-start.19 = (bf16[8,112,128]{2,1,0:T(8,128)(2,1)S(1)}, bf16[8,112,128]{2,1,0:T(8,128)(2,1)S(1)}, u32[]{:S(2)}, u32[]{:S(2)}) collective-permute-start(bf16[8,112,128]{2,1,0:T(8,128)(2,1)S(1)} %add_convert_fusion.2), channel_id=1, source_target_pairs={{0,16},{1,17},{2,18},{3,19},{4,20},{5,21},{6,22},{7,23},{8,24},{9,... | collective-permute-start | bytes 688136 | tf_op jit(solution)/shard_map/ppermute | solution.py:498
  75.9 6.9 %collective-permute-start.24 = (bf16[8,160,128]{2,1,0:T(8,128)(2,1)S(1)}, bf16[8,160,128]{2,1,0:T(8,128)(2,1)S(1)}, u32[]{:S(2)}, u32[]{:S(2)}) collective-permute-start(bf16[8,160,128]{2,1,0:T(8,128)(2,1)S(1)} %copy-done.36), channel_id=1, source_target_pairs={{0,8},{1,9},{2,10},{3,11},{4,12},{5,13},{6,14},{7,15},{8,0},{9,1},... | collective-permute-start | bytes 983048 | tf_op jit(solution)/shard_map/ppermute | solution.py:498
  77.8 16.7 %collective-permute-start.23 = (bf16[8,160,128]{2,1,0:T(8,128)(2,1)S(1)}, bf16[8,160,128]{2,1,0:T(8,128)(2,1)S(1)}, u32[]{:S(2)}, u32[]{:S(2)}) collective-permute-start(bf16[8,160,128]{2,1,0:T(8,128)(2,1)S(1)} %copy-done.35), channel_id=1, source_target_pairs={{0,8},{1,9},{2,10},{3,11},{4,12},{5,13},{6,14},{7,15},{8,0},{9,1},... | collective-permute-start | bytes 983048 | tf_op jit(solution)/shard_map/ppermute | solution.py:498
  78.3 19.3 %collective-permute-start.27 = (bf16[8,176,128]{2,1,0:T(8,128)(2,1)S(1)}, bf16[8,176,128]{2,1,0:T(8,128)(2,1)S(1)}, u32[]{:S(2)}, u32[]{:S(2)}) collective-permute-start(bf16[8,176,128]{2,1,0:T(8,128)(2,1)S(1)} %copy-done.30), channel_id=1, source_target_pairs={{0,8},{1,9},{2,10},{3,11},{4,12},{5,13},{6,14},{7,15},{8,0},{9,1},... | collective-permute-start | bytes 1081352 | tf_op jit(solution)/shard_map/ppermute | solution.py:498
  78.4 9.8 %collective-permute-start.28 = (bf16[8,176,128]{2,1,0:T(8,128)(2,1)S(1)}, bf16[8,176,128]{2,1,0:T(8,128)(2,1)S(1)}, u32[]{:S(2)}, u32[]{:S(2)}) collective-permute-start(bf16[8,176,128]{2,1,0:T(8,128)(2,1)S(1)} %copy-done.31), channel_id=1, source_target_pairs={{0,8},{1,9},{2,10},{3,11},{4,12},{5,13},{6,14},{7,15},{8,0},{9,1},... | collective-permute-start | bytes 1081352 | tf_op jit(solution)/shard_map/ppermute | solution.py:498
  83.1 11.4 %collective-permute-start.25 = (bf16[8,160,128]{2,1,0:T(8,128)(2,1)S(1)}, bf16[8,160,128]{2,1,0:T(8,128)(2,1)S(1)}, u32[]{:S(2)}, u32[]{:S(2)}) collective-permute-start(bf16[8,160,128]{2,1,0:T(8,128)(2,1)S(1)} %add_convert_fusion.1), channel_id=1, source_target_pairs={{0,16},{1,17},{2,18},{3,19},{4,20},{5,21},{6,22},{7,23},{8,24},{9,... | collective-permute-start | bytes 983048 | tf_op jit(solution)/shard_map/ppermute | solution.py:498
  88.3 10.0 %collective-permute-start.29 = (bf16[8,176,128]{2,1,0:T(8,128)(2,1)S(1)}, bf16[8,176,128]{2,1,0:T(8,128)(2,1)S(1)}, u32[]{:S(2)}, u32[]{:S(2)}) collective-permute-start(bf16[8,176,128]{2,1,0:T(8,128)(2,1)S(1)} %add_convert_fusion), channel_id=1, source_target_pairs={{0,1},{1,0},{2,3},{3,2},{4,5},{5,4},{6,7},{7,6},{8,9},{9,8},{10,11... | collective-permute-start | bytes 1081352 | tf_op jit(solution)/shard_map/ppermute | solution.py:498
  98.5 5.6 %collective-permute-start.30 = (bf16[4,176,128]{2,1,0:T(8,128)(2,1)S(1)}, bf16[4,176,128]{2,1,0:T(8,128)(2,1)S(1)}, u32[]{:S(2)}, u32[]{:S(2)}) collective-permute-start(bf16[4,176,128]{2,1,0:T(8,128)(2,1)S(1)} %slice.201), channel_id=1, source_target_pairs={{0,16},{1,17},{2,18},{3,19},{4,20},{5,21},{6,22},{7,23},{8,24},{9,... | collective-permute-start | bytes 540680 | tf_op jit(solution)/shard_map/ppermute | solution.py:498
  107.0 6.4 %collective-permute-start.33 = (bf16[336,128]{1,0:T(8,128)(2,1)S(1)}, bf16[336,128]{1,0:T(8,128)(2,1)S(1)}, u32[]{:S(2)}, u32[]{:S(2)}) collective-permute-start(bf16[336,128]{1,0:T(8,128)(2,1)S(1)} %get-tuple-element.123), channel_id=1, source_target_pairs={{0,6},{1,7},{2,4},{3,5},{4,2},{5,3},{6,0},{7,1},{8,14},{9,15},{10,... | collective-permute-start | bytes 258056 | tf_op jit(solution)/shard_map/ppermute | solution.py:498
  107.6 7.2 %collective-permute-start.32 = (bf16[336,128]{1,0:T(8,128)(2,1)S(1)}, bf16[336,128]{1,0:T(8,128)(2,1)S(1)}, u32[]{:S(2)}, u32[]{:S(2)}) collective-permute-start(bf16[336,128]{1,0:T(8,128)(2,1)S(1)} %get-tuple-element.124), channel_id=1, source_target_pairs={{0,4},{1,5},{2,6},{3,7},{4,0},{5,1},{6,2},{7,3},{8,12},{9,13},{10,... | collective-permute-start | bytes 258056 | tf_op jit(solution)/shard_map/ppermute | solution.py:498
  (53 other events, 198.4 us)
where the time goes:
time: 117 us
  starting transfers between devices  36.3 us (31%)
  waiting for transfers between devices  34.7 us (30%)
  Pallas kernels  31.3 us (27%)
  other arithmetic  6.92 us (6%)
  local copies, waits for them, and re-layouts  6.27 us (5%)
  between operations  1.27 us (1%)
    ppermute x34, starting transfers between devices, exchange(): return lax.ppermute(value, AXES, [(i, i ^ mask) for i in range(BLOCKS)])  36.3 us
    ppermute x34, waiting for transfers between devices, exchange(): return lax.ppermute(value, AXES, [(i, i ^ mask) for i in range(BLOCKS)])  34.7 us
    pallas_call x3, Pallas kernels, call(): pl.pallas_call(functools.partial(kernel, swaps), out_shape=outs, in_specs...  31.3 us
    unnamed x96, local copies, waits for them, and re-layouts  6 us
    sub x5, other arithmetic, adam_update(): return (weight - step_rate * change, first_new, second_new)  3.23 us
  transfers between devices with their start and end apart: 34, of which 17 were waited for; matrix products, arithmetic and copies ran while one was open for 6% of the time, Pallas kernels for 5%

commit v1 on v0

--- a/solution.py
+++ b/solution.py
@@ -413,30 +413,35 @@
     pack(me, flat_ref, grads, 0, 0, FIRST_ROWS)
 
 
-def shape(dims, kind):
-    return jax.ShapeDtypeStruct(dims, kind)
+def near_shape(dims, kind):
+    return pltpu.VMEM(dims, kind)
 
 
 def call(kernel, swaps, outs, scratch, cost, *operands):
     specs = [pl.BlockSpec(memory_space=pltpu.SMEM)]
     specs += [pl.BlockSpec(memory_space=pltpu.VMEM)] * (len(operands) - 1)
+    operands = [
+        pltpu.with_memory_space_constraint(operand, pltpu.VMEM) if operand.ndim == 2
+        or operand.shape[0] == 8 else operand
+        for operand in operands
+    ]
     return pl.pallas_call(
         functools.partial(kernel, swaps),
         out_shape=outs,
         in_specs=specs,
         out_specs=[pl.BlockSpec(memory_space=pltpu.VMEM)] * len(outs),
         scratch_shapes=scratch,
-        compiler_params=pltpu.CompilerParams(vmem_limit_bytes=56 * 1024 * 1024),
+        compiler_params=pltpu.CompilerParams(vmem_limit_bytes=36 * 1024 * 1024),
         cost_estimate=pl.CostEstimate(flops=cost, transcendentals=0, bytes_accessed=4_000_000),
     )(*operands)
 
 
 def attend(swaps, counts, images, pieces):
     outs = [
-        shape((D, 3 * D), BF16),
-        shape((1, GAINS + BIASES), F32),
-        shape((ROWS, 3 * D), BF16),
-        shape((ROWS, D), BF16),
+        near_shape((D, 3 * D), BF16),
+        near_shape((1, GAINS + BIASES), F32),
+        near_shape((ROWS, 3 * D), BF16),
+        near_shape((ROWS, D), BF16),
     ]
     scratch = [
         pltpu.VMEM((BLOCKS, FIRST_ROWS, LANES), F32),
@@ -446,15 +451,15 @@
 
 
 def piece_shapes(*split):
-    return [shape((8, rows, LANES), BF16) for rows in split for _ in range(4)]
+    return [near_shape((8, rows, LANES), BF16) for rows in split for _ in range(4)]
 
 
 def mlp(swaps, counts, images, upstream, attended, vec, pieces):
     outs = [
-        shape((IMGS, SEQ, D), BF16),
-        shape((ROWS, D), F32),
-        shape((1, GAINS + BIASES), F32),
-        shape((D, D), BF16),
+        jax.ShapeDtypeStruct((IMGS, SEQ, D), BF16),
+        near_shape((ROWS, D), F32),
+        near_shape((1, GAINS + BIASES), F32),
+        near_shape((D, D), BF16),
     ] + piece_shapes(*SECOND_SPLIT)
     scratch = [
         pltpu.VMEM((BLOCKS, SECOND_ROWS, LANES), F32),
@@ -478,7 +483,7 @@
 
 
 def back(swaps, counts, images, qkv, grad_mid, w_qkv, w_out, vec, vec_grad):
-    outs = [shape((IMGS, SEQ, D), BF16)] + piece_shapes(FIRST_ROWS)
+    outs = [jax.ShapeDtypeStruct((IMGS, SEQ, D), BF16)] + piece_shapes(FIRST_ROWS)
     scratch = [
         pltpu.VMEM((BLOCKS, FIRST_ROWS, LANES), F32),
         pltpu.VMEM((ROWS, D), F32),

time: 117 us -> 107 us (0.915)
  Pallas kernels: 31.3 us -> 24.2 us
  local copies, waits for them, and re-layouts: 6.27 us -> 3.4 us
    pallas_call x3, Pallas kernels: 31.3 us -> 24.2 us  [call(): pl.pallas_call(functools.partial(kernel, swaps), out_shape=outs, in_specs...]
    unnamed x96 -> x52, local copies, waits for them, and re-layouts: 6 us -> 3.13 us
  transfers between devices with their start and end apart: 34 -> 34, of which waited for: 17 -> 17; matrix products, arithmetic and copies ran while one was open for 6% -> 5% of each run, Pallas kernels for 5% -> 4%
where the time goes in v1:
time: 107 us
  starting transfers between devices  36.6 us (34%)
  waiting for transfers between devices  35.4 us (33%)
  Pallas kernels  24.2 us (23%)
  other arithmetic  5.94 us (6%)
  local copies, waits for them, and re-layouts  3.4 us (3%)
  between operations  1.17 us (1%)
    ppermute x34, starting transfers between devices, exchange(): return lax.ppermute(value, AXES, [(i, i ^ mask) for i in range(BLOCKS)])  36.6 us
    ppermute x34, waiting for transfers between devices, exchange(): return lax.ppermute(value, AXES, [(i, i ^ mask) for i in range(BLOCKS)])  35.4 us
    pallas_call x3, Pallas kernels, call(): pl.pallas_call(functools.partial(kernel, swaps), out_shape=outs, in_specs...  24.2 us
    sub x5, other arithmetic, adam_update(): return (weight - step_rate * change, first_new, second_new)  3.23 us
    unnamed x52, local copies, waits for them, and re-layouts  3.13 us
  transfers between devices with their start and end apart: 34, of which 17 were waited for; matrix products, arithmetic and copies ran while one was open for 5% of the time, Pallas kernels for 4%

profile of v1, /device:TPU:0, one launch (start us, length us, event | category | flops | bytes accessed | tf_op | source)
XLA Modules:
  0.0 106.8 jit_solution(54589399092913594)
XLA Ops:
  2.4 5.1 %collective-permute-start.8 = (bf16[336,128]{1,0:T(8,128)(2,1)S(1)}, bf16[336,128]{1,0:T(8,128)(2,1)S(1)}, u32[]{:S(2)}, u32[]{:S(2)}) collective-permute-start(bf16[336,128]{1,0:T(8,128)(2,1)S(1)} %pad_maximum_fusion.5), channel_id=1, source_target_pairs={{0,6},{1,7},{2,4},{3,5},{4,2},{5,3},{6,0},{7,1},{8,14},{9,15},{10,... | collective-permute-start | bytes 258056 | tf_op jit(solution)/shard_map/ppermute | solution.py:503
  9.9 3.8 %collective-permute-done = bf16[1,112,128]{2,1,0:T(8,128)(2,1)S(1)} collective-permute-done((bf16[1,112,128]{2,1,0:T(8,128)(2,1)S(1)}, bf16[1,112,128]{2,1,0:T(8,128)(2,1)S(1)}, u32[]{:S(2)}, u32[]{:S(2)}) %collective-permute-start) | collective-permute-done | bytes 28704 | tf_op jit(solution)/shard_map/ppermute | solution.py:503
  13.7 1.6 %collective-permute-start.1 = (bf16[2,112,128]{2,1,0:T(8,128)(2,1)S(1)}, bf16[2,112,128]{2,1,0:T(8,128)(2,1)S(1)}, u32[]{:S(2)}, u32[]{:S(2)}) collective-permute-start(bf16[2,112,128]{2,1,0:T(8,128)(2,1)S(1)} %pad_maximum_fusion.6), channel_id=1, source_target_pairs={{0,4},{1,5},{2,6},{3,7},{4,0},{5,1},{6,2},{7,3},{8,12},{9,13},{10,... | collective-permute-start | bytes 172040 | tf_op jit(solution)/shard_map/ppermute | solution.py:503
  15.3 4.0 %collective-permute-done.1 = bf16[2,112,128]{2,1,0:T(8,128)(2,1)S(1)} collective-permute-done((bf16[2,112,128]{2,1,0:T(8,128)(2,1)S(1)}, bf16[2,112,128]{2,1,0:T(8,128)(2,1)S(1)}, u32[]{:S(2)}, u32[]{:S(2)}) %collective-permute-start.1) | collective-permute-done | bytes 57376 | tf_op jit(solution)/shard_map/ppermute | solution.py:503
  19.4 1.6 %collective-permute-start.2 = (bf16[4,112,128]{2,1,0:T(8,128)(2,1)S(1)}, bf16[4,112,128]{2,1,0:T(8,128)(2,1)S(1)}, u32[]{:S(2)}, u32[]{:S(2)}) collective-permute-start(bf16[4,112,128]{2,1,0:T(8,128)(2,1)S(1)} %pad_maximum_fusion.4), channel_id=1, source_target_pairs={{0,1},{1,0},{2,3},{3,2},{4,5},{5,4},{6,7},{7,6},{8,9},{9,8},{10,11... | collective-permute-start | bytes 344072 | tf_op jit(solution)/shard_map/ppermute | solution.py:503
  21.7 1.6 %collective-permute-start.13 = (bf16[4,176,128]{2,1,0:T(8,128)(2,1)S(1)}, bf16[4,176,128]{2,1,0:T(8,128)(2,1)S(1)}, u32[]{:S(2)}, u32[]{:S(2)}) collective-permute-start(bf16[4,176,128]{2,1,0:T(8,128)(2,1)S(1)} %pad_maximum_fusion.2), channel_id=1, source_target_pairs={{0,16},{1,17},{2,18},{3,19},{4,20},{5,21},{6,22},{7,23},{8,24},{9,... | collective-permute-start | bytes 540680 | tf_op jit(solution)/shard_map/ppermute | solution.py:503
  24.3 1.6 %collective-permute-start.3 = (bf16[8,112,128]{2,1,0:T(8,128)(2,1)S(1)}, bf16[8,112,128]{2,1,0:T(8,128)(2,1)S(1)}, u32[]{:S(2)}, u32[]{:S(2)}) collective-permute-start(bf16[8,112,128]{2,1,0:T(8,128)(2,1)S(1)} %pad_maximum_fusion.1.refs_0_), channel_id=1, source_target_pairs={{0,16},{1,17},{2,18},{3,19},{4,20},{5,21},{6,22},{7,23},{8,24},{9,... | collective-permute-start | bytes 688136 | tf_op jit(solution)/shard_map/ppermute | solution.py:503
  25.9 2.2 %collective-permute-done.13 = bf16[4,176,128]{2,1,0:T(8,128)(2,1)S(1)} collective-permute-done((bf16[4,176,128]{2,1,0:T(8,128)(2,1)S(1)}, bf16[4,176,128]{2,1,0:T(8,128)(2,1)S(1)}, u32[]{:S(2)}, u32[]{:S(2)}) %collective-permute-start.13) | collective-permute-done | bytes 180256 | tf_op jit(solution)/shard_map/ppermute | solution.py:503
  28.1 2.6 %collective-permute-start.14 = (bf16[8,176,128]{2,1,0:T(8,128)(2,1)S(1)}, bf16[8,176,128]{2,1,0:T(8,128)(2,1)S(1)}, u32[]{:S(2)}, u32[]{:S(2)}) collective-permute-start(bf16[8,176,128]{2,1,0:T(8,128)(2,1)S(1)} %constant_dynamic-update-slice_fusion.5.refs_4_), channel_id=1, source_target_pairs={{0,1},{1,0},{2,3},{3,2},{4,5},{5,4},{6,7},{7,6},{8,9},{9,8},{10,11... | collective-permute-start | bytes 1081352 | tf_op jit(solution)/shard_map/ppermute | solution.py:503
  30.7 1.6 %collective-permute-start.10 = (bf16[8,160,128]{2,1,0:T(8,128)(2,1)S(1)}, bf16[8,160,128]{2,1,0:T(8,128)(2,1)S(1)}, u32[]{:S(2)}, u32[]{:S(2)}) collective-permute-start(bf16[8,160,128]{2,1,0:T(8,128)(2,1)S(1)} %constant_dynamic-update-slice_fusion.refs_0_), channel_id=1, source_target_pairs={{0,16},{1,17},{2,18},{3,19},{4,20},{5,21},{6,22},{7,23},{8,24},{9,... | collective-permute-start | bytes 983048 | tf_op jit(solution)/shard_map/ppermute | solution.py:503
  33.9 4.0 %collective-permute-done.10.refs_1_ = bf16[8,160,128]{2,1,0:T(8,128)(2,1)S(1)} collective-permute-done((bf16[8,160,128]{2,1,0:T(8,128)(2,1)S(1)}, bf16[8,160,128]{2,1,0:T(8,128)(2,1)S(1)}, u32[]{:S(2)}, u32[]{:S(2)}) %collective-permute-start.10) | collective-permute-done | bytes 327712 | tf_op jit(solution)/shard_map/ppermute | solution.py:503
  38.4 4.8 %shard_map.404 = (bf16[384,1152]{1,0:T(8,128)(2,1)S(1)}, f32[1,4608]{1,0:T(1,128)S(1)}, bf16[416,1152]{1,0:T(8,128)(2,1)S(1)}, bf16[416,384]{1,0:T(8,128)(2,1)S(1)}) custom-call(s32[32]{0:T(128)S(1)} %copy-done, bf16[2,197,384]{2,1,0:T(8,128)(2,1)S(1)} %copy.48.x_ref, bf16[8,112,128]{2,1,0:T(8,128)(2,1)S(1)} %pad_maximum_fusion.1.refs_0_, ...), custom_call_target="tpu_custom_call" | custom-call | flops 5000000000 | bytes 4000000 | tf_op jit(solution)/shard_map/pallas_call | solution.py:428
  43.2 11.8 %shard_map.405 = (bf16[2,197,384]{2,1,0:T(8,128)(2,1)S(1)}, f32[416,384]{1,0:T(8,128)S(1)}, f32[1,4608]{1,0:T(1,128)S(1)}, bf16[384,384]{1,0:T(8,128)(2,1)S(1)},...) custom-call(s32[32]{0:T(128)S(1)} %copy-done, ...), custom_call_target="tpu_custom_call" | custom-call | flops 8000000000 | bytes 4000000 | tf_op jit(solution)/shard_map/pallas_call | solution.py:428
  55.0 7.7 %shard_map.406 = (bf16[2,197,384]{2,1,0:T(8,128)(2,1)S(1)}, bf16[8,112,128]{2,1,0:T(8,128)(2,1)S(1)}, bf16[8,112,128]{2,1,0:T(8,128)(2,1)S(1)}, bf16[8,112,128]{2,1,0:T(8,128)(2,1)S(1)}, bf16[8,112,128]{2,1,0:T(8,128)(2,1)S(1)}) custom-call(s32[32]{0:T(128)S(1)} %copy-done, bf16[2,197,384]{2,1,0:T(8,128)(2,1)S(1)} %copy.48.x_ref, ...), custom_call_target="tpu_custom_call" | custom-call | flops 6000000000 | bytes 4000000 | tf_op jit(solution)/shard_map/pallas_call | solution.py:428
  64.3 1.6 %collective-permute-start.19 = (bf16[8,112,128]{2,1,0:T(8,128)(2,1)S(1)}, bf16[8,112,128]{2,1,0:T(8,128)(2,1)S(1)}, u32[]{:S(2)}, u32[]{:S(2)}) collective-permute-start(bf16[8,112,128]{2,1,0:T(8,128)(2,1)S(1)} %add_convert_fusion.2), channel_id=1, source_target_pairs={{0,16},{1,17},{2,18},{3,19},{4,20},{5,21},{6,22},{7,23},{8,24},{9,... | collective-permute-start | bytes 688136 | tf_op jit(solution)/shard_map/ppermute | solution.py:503
  68.8 3.2 %collective-permute-done.19 = bf16[8,112,128]{2,1,0:T(8,128)(2,1)S(1)} collective-permute-done((bf16[8,112,128]{2,1,0:T(8,128)(2,1)S(1)}, bf16[8,112,128]{2,1,0:T(8,128)(2,1)S(1)}, u32[]{:S(2)}, u32[]{:S(2)}) %collective-permute-start.19) | collective-permute-done | bytes 229408 | tf_op jit(solution)/shard_map/ppermute | solution.py:503
  72.9 1.6 %collective-permute-start.25 = (bf16[8,160,128]{2,1,0:T(8,128)(2,1)S(1)}, bf16[8,160,128]{2,1,0:T(8,128)(2,1)S(1)}, u32[]{:S(2)}, u32[]{:S(2)}) collective-permute-start(bf16[8,160,128]{2,1,0:T(8,128)(2,1)S(1)} %add_convert_fusion.1), channel_id=1, source_target_pairs={{0,16},{1,17},{2,18},{3,19},{4,20},{5,21},{6,22},{7,23},{8,24},{9,... | collective-permute-start | bytes 983048 | tf_op jit(solution)/shard_map/ppermute | solution.py:503
  74.4 2.6 %collective-permute-done.20 = bf16[4,112,128]{2,1,0:T(8,128)(2,1)S(1)} collective-permute-done((bf16[4,112,128]{2,1,0:T(8,128)(2,1)S(1)}, bf16[4,112,128]{2,1,0:T(8,128)(2,1)S(1)}, u32[]{:S(2)}, u32[]{:S(2)}) %collective-permute-start.20) | collective-permute-done | bytes 114720 | tf_op jit(solution)/shard_map/ppermute | solution.py:503
  79.3 2.9 %collective-permute-done.21 = bf16[2,112,128]{2,1,0:T(8,128)(2,1)S(1)} collective-permute-done((bf16[2,112,128]{2,1,0:T(8,128)(2,1)S(1)}, bf16[2,112,128]{2,1,0:T(8,128)(2,1)S(1)}, u32[]{:S(2)}, u32[]{:S(2)}) %collective-permute-start.21) | collective-permute-done | bytes 57376 | tf_op jit(solution)/shard_map/ppermute | solution.py:503
  82.2 2.3 %collective-permute-start.22 = (bf16[1,112,128]{2,1,0:T(8,128)(2,1)S(1)}, bf16[1,112,128]{2,1,0:T(8,128)(2,1)S(1)}, u32[]{:S(2)}, u32[]{:S(2)}) collective-permute-start(bf16[1,112,128]{2,1,0:T(8,128)(2,1)S(1)} %slice.205), channel_id=1, source_target_pairs={{0,2},{1,3},{2,0},{3,1},{4,6},{5,7},{6,4},{7,5},{8,10},{9,11},{10,... | collective-permute-start | bytes 86024 | tf_op jit(solution)/shard_map/ppermute | solution.py:503
  88.5 1.6 %collective-permute-start.30 = (bf16[4,176,128]{2,1,0:T(8,128)(2,1)S(1)}, bf16[4,176,128]{2,1,0:T(8,128)(2,1)S(1)}, u32[]{:S(2)}, u32[]{:S(2)}) collective-permute-start(bf16[4,176,128]{2,1,0:T(8,128)(2,1)S(1)} %slice.201), channel_id=1, source_target_pairs={{0,16},{1,17},{2,18},{3,19},{4,20},{5,21},{6,22},{7,23},{8,24},{9,... | collective-permute-start | bytes 540680 | tf_op jit(solution)/shard_map/ppermute | solution.py:503
  90.1 3.9 %collective-permute-done.30 = bf16[4,176,128]{2,1,0:T(8,128)(2,1)S(1)} collective-permute-done((bf16[4,176,128]{2,1,0:T(8,128)(2,1)S(1)}, bf16[4,176,128]{2,1,0:T(8,128)(2,1)S(1)}, u32[]{:S(2)}, u32[]{:S(2)}) %collective-permute-start.30) | collective-permute-done | bytes 180256 | tf_op jit(solution)/shard_map/ppermute | solution.py:503
  94.1 2.9 %collective-permute-start.31 = (bf16[336,128]{1,0:T(8,128)(2,1)S(1)}, bf16[336,128]{1,0:T(8,128)(2,1)S(1)}, u32[]{:S(2)}, u32[]{:S(2)}) collective-permute-start(bf16[336,128]{1,0:T(8,128)(2,1)S(1)} %get-tuple-element.122), channel_id=1, source_target_pairs={{0,2},{1,3},{2,0},{3,1},{4,6},{5,7},{6,4},{7,5},{8,10},{9,11},{10,... | collective-permute-start | bytes 258056 | tf_op jit(solution)/shard_map/ppermute | solution.py:503
  99.5 3.9 %collective-permute-done.33 = bf16[336,128]{1,0:T(8,128)(2,1)S(1)} collective-permute-done((bf16[336,128]{1,0:T(8,128)(2,1)S(1)}, bf16[336,128]{1,0:T(8,128)(2,1)S(1)}, u32[]{:S(2)}, u32[]{:S(2)}) %collective-permute-start.33) | collective-permute-done | bytes 86048 | tf_op jit(solution)/shard_map/ppermute | solution.py:503
  (149 shorter events, 25.4 us)
Async XLA Ops:
  2.4 18.6 %collective-permute-start.8 = (bf16[336,128]{1,0:T(8,128)(2,1)S(1)}, bf16[336,128]{1,0:T(8,128)(2,1)S(1)}, u32[]{:S(2)}, u32[]{:S(2)}) collective-permute-start(bf16[336,128]{1,0:T(8,128)(2,1)S(1)} %pad_maximum_fusion.5), channel_id=1, source_target_pairs={{0,6},{1,7},{2,4},{3,5},{4,2},{5,3},{6,0},{7,1},{8,14},{9,15},{10,... | collective-permute-start | bytes 258056 | tf_op jit(solution)/shard_map/ppermute | solution.py:503
  7.6 13.4 %collective-permute-start.7 = (bf16[336,128]{1,0:T(8,128)(2,1)S(1)}, bf16[336,128]{1,0:T(8,128)(2,1)S(1)}, u32[]{:S(2)}, u32[]{:S(2)}) collective-permute-start(bf16[336,128]{1,0:T(8,128)(2,1)S(1)} %pad_maximum_fusion.5), channel_id=1, source_target_pairs={{0,4},{1,5},{2,6},{3,7},{4,0},{5,1},{6,2},{7,3},{8,12},{9,13},{10,... | collective-permute-start | bytes 258056 | tf_op jit(solution)/shard_map/ppermute | solution.py:503
  7.6 13.5 %collective-permute-start.6 = (bf16[336,128]{1,0:T(8,128)(2,1)S(1)}, bf16[336,128]{1,0:T(8,128)(2,1)S(1)}, u32[]{:S(2)}, u32[]{:S(2)}) collective-permute-start(bf16[336,128]{1,0:T(8,128)(2,1)S(1)} %pad_maximum_fusion.5), channel_id=1, source_target_pairs={{0,2},{1,3},{2,0},{3,1},{4,6},{5,7},{6,4},{7,5},{8,10},{9,11},{10,... | collective-permute-start | bytes 258056 | tf_op jit(solution)/shard_map/ppermute | solution.py:503
  13.7 5.7 %collective-permute-start.1 = (bf16[2,112,128]{2,1,0:T(8,128)(2,1)S(1)}, bf16[2,112,128]{2,1,0:T(8,128)(2,1)S(1)}, u32[]{:S(2)}, u32[]{:S(2)}) collective-permute-start(bf16[2,112,128]{2,1,0:T(8,128)(2,1)S(1)} %pad_maximum_fusion.6), channel_id=1, source_target_pairs={{0,4},{1,5},{2,6},{3,7},{4,0},{5,1},{6,2},{7,3},{8,12},{9,13},{10,... | collective-permute-start | bytes 172040 | tf_op jit(solution)/shard_map/ppermute | solution.py:503
  21.1 9.6 %collective-permute-start.9 = (bf16[4,160,128]{2,1,0:T(8,128)(2,1)S(1)}, bf16[4,160,128]{2,1,0:T(8,128)(2,1)S(1)}, u32[]{:S(2)}, u32[]{:S(2)}) collective-permute-start(bf16[4,160,128]{2,1,0:T(8,128)(2,1)S(1)} %pad_maximum_fusion.3), channel_id=1, source_target_pairs={{0,1},{1,0},{2,3},{3,2},{4,5},{5,4},{6,7},{7,6},{8,9},{9,8},{10,11... | collective-permute-start | bytes 491528 | tf_op jit(solution)/shard_map/ppermute | solution.py:503
  21.7 6.4 %collective-permute-start.13 = (bf16[4,176,128]{2,1,0:T(8,128)(2,1)S(1)}, bf16[4,176,128]{2,1,0:T(8,128)(2,1)S(1)}, u32[]{:S(2)}, u32[]{:S(2)}) collective-permute-start(bf16[4,176,128]{2,1,0:T(8,128)(2,1)S(1)} %pad_maximum_fusion.2), channel_id=1, source_target_pairs={{0,16},{1,17},{2,18},{3,19},{4,20},{5,21},{6,22},{7,23},{8,24},{9,... | collective-permute-start | bytes 540680 | tf_op jit(solution)/shard_map/ppermute | solution.py:503
  24.3 8.7 %collective-permute-start.3 = (bf16[8,112,128]{2,1,0:T(8,128)(2,1)S(1)}, bf16[8,112,128]{2,1,0:T(8,128)(2,1)S(1)}, u32[]{:S(2)}, u32[]{:S(2)}) collective-permute-start(bf16[8,112,128]{2,1,0:T(8,128)(2,1)S(1)} %pad_maximum_fusion.1.refs_0_), channel_id=1, source_target_pairs={{0,16},{1,17},{2,18},{3,19},{4,20},{5,21},{6,22},{7,23},{8,24},{9,... | collective-permute-start | bytes 688136 | tf_op jit(solution)/shard_map/ppermute | solution.py:503
  28.1 9.8 %collective-permute-start.14 = (bf16[8,176,128]{2,1,0:T(8,128)(2,1)S(1)}, bf16[8,176,128]{2,1,0:T(8,128)(2,1)S(1)}, u32[]{:S(2)}, u32[]{:S(2)}) collective-permute-start(bf16[8,176,128]{2,1,0:T(8,128)(2,1)S(1)} %constant_dynamic-update-slice_fusion.5.refs_4_), channel_id=1, source_target_pairs={{0,1},{1,0},{2,3},{3,2},{4,5},{5,4},{6,7},{7,6},{8,9},{9,8},{10,11... | collective-permute-start | bytes 1081352 | tf_op jit(solution)/shard_map/ppermute | solution.py:503
  30.7 7.1 %collective-permute-start.10 = (bf16[8,160,128]{2,1,0:T(8,128)(2,1)S(1)}, bf16[8,160,128]{2,1,0:T(8,128)(2,1)S(1)}, u32[]{:S(2)}, u32[]{:S(2)}) collective-permute-start(bf16[8,160,128]{2,1,0:T(8,128)(2,1)S(1)} %constant_dynamic-update-slice_fusion.refs_0_), channel_id=1, source_target_pairs={{0,16},{1,17},{2,18},{3,19},{4,20},{5,21},{6,22},{7,23},{8,24},{9,... | collective-permute-start | bytes 983048 | tf_op jit(solution)/shard_map/ppermute | solution.py:503
  33.0 5.4 %collective-permute-start.5 = (bf16[8,112,128]{2,1,0:T(8,128)(2,1)S(1)}, bf16[8,112,128]{2,1,0:T(8,128)(2,1)S(1)}, u32[]{:S(2)}, u32[]{:S(2)}) collective-permute-start(bf16[8,112,128]{2,1,0:T(8,128)(2,1)S(1)} %collective-permute-done.3.refs_1_), channel_id=1, source_target_pairs={{0,8},{1,9},{2,10},{3,11},{4,12},{5,13},{6,14},{7,15},{8,0},{9,1},... | collective-permute-start | bytes 688136 | tf_op jit(solution)/shard_map/ppermute | solution.py:503
  33.1 10.1 %collective-permute-start.11 = (bf16[8,160,128]{2,1,0:T(8,128)(2,1)S(1)}, bf16[8,160,128]{2,1,0:T(8,128)(2,1)S(1)}, u32[]{:S(2)}, u32[]{:S(2)}) collective-permute-start(bf16[8,160,128]{2,1,0:T(8,128)(2,1)S(1)} %constant_dynamic-update-slice_fusion.refs_0_), channel_id=1, source_target_pairs={{0,8},{1,9},{2,10},{3,11},{4,12},{5,13},{6,14},{7,15},{8,0},{9,1},... | collective-permute-start | bytes 983048 | tf_op jit(solution)/shard_map/ppermute | solution.py:503
  33.8 9.4 %collective-permute-start.15 = (bf16[8,176,128]{2,1,0:T(8,128)(2,1)S(1)}, bf16[8,176,128]{2,1,0:T(8,128)(2,1)S(1)}, u32[]{:S(2)}, u32[]{:S(2)}) collective-permute-start(bf16[8,176,128]{2,1,0:T(8,128)(2,1)S(1)} %constant_dynamic-update-slice_fusion.5.refs_4_), channel_id=1, source_target_pairs={{0,8},{1,9},{2,10},{3,11},{4,12},{5,13},{6,14},{7,15},{8,0},{9,1},... | collective-permute-start | bytes 1081352 | tf_op jit(solution)/shard_map/ppermute | solution.py:503
  62.8 5.5 %collective-permute-start.17 = (bf16[8,112,128]{2,1,0:T(8,128)(2,1)S(1)}, bf16[8,112,128]{2,1,0:T(8,128)(2,1)S(1)}, u32[]{:S(2)}, u32[]{:S(2)}) collective-permute-start(bf16[8,112,128]{2,1,0:T(8,128)(2,1)S(1)} %get-tuple-element.57), channel_id=1, source_target_pairs={{0,8},{1,9},{2,10},{3,11},{4,12},{5,13},{6,14},{7,15},{8,0},{9,1},... | collective-permute-start | bytes 688136 | tf_op jit(solution)/shard_map/ppermute | solution.py:503
  64.3 7.7 %collective-permute-start.19 = (bf16[8,112,128]{2,1,0:T(8,128)(2,1)S(1)}, bf16[8,112,128]{2,1,0:T(8,128)(2,1)S(1)}, u32[]{:S(2)}, u32[]{:S(2)}) collective-permute-start(bf16[8,112,128]{2,1,0:T(8,128)(2,1)S(1)} %add_convert_fusion.2), channel_id=1, source_target_pairs={{0,16},{1,17},{2,18},{3,19},{4,20},{5,21},{6,22},{7,23},{8,24},{9,... | collective-permute-start | bytes 688136 | tf_op jit(solution)/shard_map/ppermute | solution.py:503
  65.9 6.9 %collective-permute-start.24 = (bf16[8,160,128]{2,1,0:T(8,128)(2,1)S(1)}, bf16[8,160,128]{2,1,0:T(8,128)(2,1)S(1)}, u32[]{:S(2)}, u32[]{:S(2)}) collective-permute-start(bf16[8,160,128]{2,1,0:T(8,128)(2,1)S(1)} %get-tuple-element.63), channel_id=1, source_target_pairs={{0,8},{1,9},{2,10},{3,11},{4,12},{5,13},{6,14},{7,15},{8,0},{9,1},... | collective-permute-start | bytes 983048 | tf_op jit(solution)/shard_map/ppermute | solution.py:503
  67.8 16.7 %collective-permute-start.23 = (bf16[8,160,128]{2,1,0:T(8,128)(2,1)S(1)}, bf16[8,160,128]{2,1,0:T(8,128)(2,1)S(1)}, u32[]{:S(2)}, u32[]{:S(2)}) collective-permute-start(bf16[8,160,128]{2,1,0:T(8,128)(2,1)S(1)} %get-tuple-element.61), channel_id=1, source_target_pairs={{0,8},{1,9},{2,10},{3,11},{4,12},{5,13},{6,14},{7,15},{8,0},{9,1},... | collective-permute-start | bytes 983048 | tf_op jit(solution)/shard_map/ppermute | solution.py:503
  68.3 20.0 %collective-permute-start.27 = (bf16[8,176,128]{2,1,0:T(8,128)(2,1)S(1)}, bf16[8,176,128]{2,1,0:T(8,128)(2,1)S(1)}, u32[]{:S(2)}, u32[]{:S(2)}) collective-permute-start(bf16[8,176,128]{2,1,0:T(8,128)(2,1)S(1)} %get-tuple-element.65), channel_id=1, source_target_pairs={{0,8},{1,9},{2,10},{3,11},{4,12},{5,13},{6,14},{7,15},{8,0},{9,1},... | collective-permute-start | bytes 1081352 | tf_op jit(solution)/shard_map/ppermute | solution.py:503
  68.3 9.9 %collective-permute-start.28 = (bf16[8,176,128]{2,1,0:T(8,128)(2,1)S(1)}, bf16[8,176,128]{2,1,0:T(8,128)(2,1)S(1)}, u32[]{:S(2)}, u32[]{:S(2)}) collective-permute-start(bf16[8,176,128]{2,1,0:T(8,128)(2,1)S(1)} %get-tuple-element.67), channel_id=1, source_target_pairs={{0,8},{1,9},{2,10},{3,11},{4,12},{5,13},{6,14},{7,15},{8,0},{9,1},... | collective-permute-start | bytes 1081352 | tf_op jit(solution)/shard_map/ppermute | solution.py:503
  72.9 11.6 %collective-permute-start.25 = (bf16[8,160,128]{2,1,0:T(8,128)(2,1)S(1)}, bf16[8,160,128]{2,1,0:T(8,128)(2,1)S(1)}, u32[]{:S(2)}, u32[]{:S(2)}) collective-permute-start(bf16[8,160,128]{2,1,0:T(8,128)(2,1)S(1)} %add_convert_fusion.1), channel_id=1, source_target_pairs={{0,16},{1,17},{2,18},{3,19},{4,20},{5,21},{6,22},{7,23},{8,24},{9,... | collective-permute-start | bytes 983048 | tf_op jit(solution)/shard_map/ppermute | solution.py:503
  78.3 10.0 %collective-permute-start.29 = (bf16[8,176,128]{2,1,0:T(8,128)(2,1)S(1)}, bf16[8,176,128]{2,1,0:T(8,128)(2,1)S(1)}, u32[]{:S(2)}, u32[]{:S(2)}) collective-permute-start(bf16[8,176,128]{2,1,0:T(8,128)(2,1)S(1)} %add_convert_fusion), channel_id=1, source_target_pairs={{0,1},{1,0},{2,3},{3,2},{4,5},{5,4},{6,7},{7,6},{8,9},{9,8},{10,11... | collective-permute-start | bytes 1081352 | tf_op jit(solution)/shard_map/ppermute | solution.py:503
  84.7 5.4 %collective-permute-start.26 = (bf16[4,160,128]{2,1,0:T(8,128)(2,1)S(1)}, bf16[4,160,128]{2,1,0:T(8,128)(2,1)S(1)}, u32[]{:S(2)}, u32[]{:S(2)}) collective-permute-start(bf16[4,160,128]{2,1,0:T(8,128)(2,1)S(1)} %slice.202), channel_id=1, source_target_pairs={{0,1},{1,0},{2,3},{3,2},{4,5},{5,4},{6,7},{7,6},{8,9},{9,8},{10,11... | collective-permute-start | bytes 491528 | tf_op jit(solution)/shard_map/ppermute | solution.py:503
  88.5 5.6 %collective-permute-start.30 = (bf16[4,176,128]{2,1,0:T(8,128)(2,1)S(1)}, bf16[4,176,128]{2,1,0:T(8,128)(2,1)S(1)}, u32[]{:S(2)}, u32[]{:S(2)}) collective-permute-start(bf16[4,176,128]{2,1,0:T(8,128)(2,1)S(1)} %slice.201), channel_id=1, source_target_pairs={{0,16},{1,17},{2,18},{3,19},{4,20},{5,21},{6,22},{7,23},{8,24},{9,... | collective-permute-start | bytes 540680 | tf_op jit(solution)/shard_map/ppermute | solution.py:503
  97.0 6.4 %collective-permute-start.33 = (bf16[336,128]{1,0:T(8,128)(2,1)S(1)}, bf16[336,128]{1,0:T(8,128)(2,1)S(1)}, u32[]{:S(2)}, u32[]{:S(2)}) collective-permute-start(bf16[336,128]{1,0:T(8,128)(2,1)S(1)} %get-tuple-element.123), channel_id=1, source_target_pairs={{0,6},{1,7},{2,4},{3,5},{4,2},{5,3},{6,0},{7,1},{8,14},{9,15},{10,... | collective-permute-start | bytes 258056 | tf_op jit(solution)/shard_map/ppermute | solution.py:503
  97.6 7.2 %collective-permute-start.32 = (bf16[336,128]{1,0:T(8,128)(2,1)S(1)}, bf16[336,128]{1,0:T(8,128)(2,1)S(1)}, u32[]{:S(2)}, u32[]{:S(2)}) collective-permute-start(bf16[336,128]{1,0:T(8,128)(2,1)S(1)} %get-tuple-element.124), channel_id=1, source_target_pairs={{0,4},{1,5},{2,6},{3,7},{4,0},{5,1},{6,2},{7,3},{8,12},{9,13},{10,... | collective-permute-start | bytes 258056 | tf_op jit(solution)/shard_map/ppermute | solution.py:503
  (31 other events, 110.5 us)

commit v2 on v1

--- a/solution.py
+++ b/solution.py
@@ -44,8 +44,9 @@
 BIAS_ROW = QKV_ROWS
 GAIN_ROW = BIAS_ROW + 1
 FIRST_ROWS = 112
-SECOND_SPLIT = (160, 176)
-SECOND_ROWS = sum(SECOND_SPLIT)
+SECOND_ROWS = 336
+GATHER_SPLIT = (144, 192)
+SUM_SPLIT = (192, 144)
 OUT_START = FC_ROWS
 FC2_START = OUT_START + OUT_ROWS
 GAINS = 2 * D
@@ -54,6 +55,7 @@
 BIAS_PART = BIASES // BLOCKS
 CHUNKS = FF // D
 Y_BIT, Z_LOW, Z_HIGH, CORE_BIT, X_BIT = 1, 2, 4, 8, 16
+LINE = (Z_LOW, Z_HIGH, Z_LOW + Z_HIGH)
 
 
 def nn(a, b):
@@ -237,8 +239,8 @@
     me = position(swaps)
     count = counts_ref[lax.axis_index(AXES)]
     live = [jnp.where(count > b, 1.0, 0.0).astype(F32) for b in range(IMGS)]
-    unpack(me, pieces[:4], flat_ref, 0, 0, SECOND_SPLIT[0])
-    unpack(me, pieces[4:], flat_ref, 1, *SECOND_SPLIT)
+    unpack(me, pieces[:4], flat_ref, 0, 0, GATHER_SPLIT[0])
+    unpack(me, pieces[4:], flat_ref, 1, *GATHER_SPLIT)
 
     def quads(quad, carry):
         rows = pl.ds(pl.multiple_of(quad * 4 * STRIPE, 16), 4 * STRIPE)
@@ -333,8 +335,8 @@
     lax.fori_loop(0, BLOCKS, talls_back, 0)
     used = FC2_START + FC_ROWS
     flat_ref[:, used:, :] = jnp.zeros((BLOCKS, SECOND_ROWS - used, LANES), F32)
-    pack(me, flat_ref, grads[:4], 0, 0, SECOND_SPLIT[0])
-    pack(me, flat_ref, grads[4:], 1, *SECOND_SPLIT)
+    pack(me, flat_ref, grads[:4], 0, 0, SUM_SPLIT[0])
+    pack(me, flat_ref, grads[4:], 1, *SUM_SPLIT)
 
 
 def back_kernel(
@@ -460,7 +462,7 @@
         near_shape((ROWS, D), F32),
         near_shape((1, GAINS + BIASES), F32),
         near_shape((D, D), BF16),
-    ] + piece_shapes(*SECOND_SPLIT)
+    ] + piece_shapes(*SUM_SPLIT)
     scratch = [
         pltpu.VMEM((BLOCKS, SECOND_ROWS, LANES), F32),
         pltpu.VMEM((CHUNKS, D, D), BF16),
@@ -504,9 +506,11 @@
 
 
 def gather_line(block):
-    held = block[None]
-    for mask in (Z_LOW, Z_HIGH, Y_BIT):
-        held = jnp.concatenate([held, exchange(held, mask)])
+    line = [block]
+    for mask in LINE:
+        line.append(exchange(block, mask))
+    held = jnp.stack(line)
+    held = jnp.concatenate([held, exchange(held, Y_BIT)])
     other = exchange(held, X_BIT)
     core = exchange(held, CORE_BIT)
     last = exchange(other, CORE_BIT)
@@ -520,16 +524,21 @@
     crossed = exchange(far_sum.astype(BF16), X_BIT)
     from_core = exchange(send, CORE_BIT)
     held = keep.astype(F32) + from_core.astype(F32) + crossed.astype(F32)
-    for mask in (Y_BIT, Z_HIGH, Z_LOW):
-        half = held.shape[0] // 2
-        crossed = exchange(held[half:].astype(BF16), mask)
-        held = held[:half] + crossed.astype(F32)
-    return held[0]
+    crossed = exchange(held[4:].astype(BF16), Y_BIT)
+    return sum_line(held[:4] + crossed.astype(F32))
+
+
+def sum_line(line):
+    total = line[0]
+    for step, mask in enumerate(LINE):
+        crossed = exchange(line[step + 1].astype(BF16), mask)
+        total = total + crossed.astype(F32)
+    return total
 
 
 def gather_blocks(block, split):
     line = [block]
-    for mask in (Z_LOW, Z_HIGH, Z_LOW + Z_HIGH):
+    for mask in LINE:
         line.append(exchange(block, mask))
     colors = []
     for color, (near, far) in enumerate(((Y_BIT, X_BIT), (X_BIT, Y_BIT))):
@@ -558,11 +567,7 @@
         crossed = exchange(plane[4:].astype(BF16), near)
         done.append(plane[:4] + crossed.astype(F32))
     line = jnp.concatenate(done, axis=1)
-    total = line[0]
-    for step, mask in ((1, Z_LOW), (2, Z_HIGH), (3, Z_LOW + Z_HIGH)):
-        crossed = exchange(line[step].astype(BF16), mask)
-        total = total + crossed.astype(F32)
-    return total
+    return sum_line(line)
 
 
 def ordered_pieces(whole, split):
@@ -638,18 +643,18 @@
 
 def device_step(devices, images, counts, upstream, *state):
     masters, firsts, seconds = state[:6], state[6:12], state[12:18]
-    lowered = [master.astype(BF16) for master in masters]
     swaps = devices == BLOCKS
     if swaps:
-        qkv, out, fc1, fc2, gains, biases = lowered
-        first = gather_line(build_first(qkv, gains, biases))
-        second = gather_blocks(build_second(out, fc1, fc2), SECOND_SPLIT)
+        qkv, out, fc1, fc2, gains, biases = masters
+        first = gather_line(build_first(qkv, gains, biases).astype(BF16))
+        second = gather_blocks(build_second(out, fc1, fc2).astype(BF16), GATHER_SPLIT)
     else:
         qkv, out, fc1, fc2, gains, biases = [
-            lax.all_gather(part, AXES, axis=0, tiled=True).reshape(BLOCKS, -1) for part in lowered
+            lax.all_gather(part.astype(BF16), AXES, axis=0, tiled=True).reshape(BLOCKS, -1)
+            for part in masters
         ]
         first = ordered_pieces(build_first(qkv, gains, biases), (FIRST_ROWS,))
-        second = ordered_pieces(build_second(out, fc1, fc2), SECOND_SPLIT)
+        second = ordered_pieces(build_second(out, fc1, fc2), GATHER_SPLIT)
     w_qkv, vec, qkv, attended = attend(swaps, counts, images, first)
     block_out, grad_mid, vec_grad, w_out, *second_grads = mlp(
         swaps, counts, images, upstream, attended, vec, second

time: 107 us -> 102 us (0.953)
  waiting for transfers between devices: 35.4 us -> 30.5 us
  starting transfers between devices: 36.6 us -> 37.9 us
    ppermute x34 -> x36, waiting for transfers between devices: 35.4 us -> 30.5 us  [exchange(): return lax.ppermute(value, AXES, [(i, i ^ mask) for i in range(BLOCKS)])]
    ppermute x34 -> x36, starting transfers between devices: 36.6 us -> 37.9 us  [exchange(): return lax.ppermute(value, AXES, [(i, i ^ mask) for i in range(BLOCKS)])]
    unnamed x52 -> x55, local copies, waits for them, and re-layouts: 3.13 us -> 3.07 us
  transfers between devices with their start and end apart: 34 -> 36, of which waited for: 17 -> 14; matrix products, arithmetic and copies ran while one was open for 5% -> 5% of each run, Pallas kernels for 4% -> 5%
where the time goes in v2:
time: 102 us
  starting transfers between devices  37.9 us (37%)
  waiting for transfers between devices  30.5 us (30%)
  Pallas kernels  24.2 us (24%)
  other arithmetic  5.14 us (5%)
  local copies, waits for them, and re-layouts  3.35 us (3%)
  between operations  1.21 us (1%)
    ppermute x36, starting transfers between devices, exchange(): return lax.ppermute(value, AXES, [(i, i ^ mask) for i in range(BLOCKS)])  37.9 us
    ppermute x36, waiting for transfers between devices, exchange(): return lax.ppermute(value, AXES, [(i, i ^ mask) for i in range(BLOCKS)])  30.5 us
    pallas_call x3, Pallas kernels, call(): pl.pallas_call(functools.partial(kernel, swaps), out_shape=outs, in_specs...  24.2 us
    sub x5, other arithmetic, adam_update(): return (weight - step_rate * change, first_new, second_new)  3.23 us
    unnamed x55, local copies, waits for them, and re-layouts  3.07 us
  transfers between devices with their start and end apart: 36, of which 14 were waited for; matrix products, arithmetic and copies ran while one was open for 5% of the time, Pallas kernels for 5%

profile of v2, /device:TPU:0, one launch (start us, length us, event | category | flops | bytes accessed | tf_op | source)
XLA Modules:
  0.0 102.2 jit_solution(4406797517961225306)
XLA Ops:
  1.8 5.1 %collective-permute-start.2 = (bf16[112,128]{1,0:T(8,128)(2,1)S(1)}, bf16[112,128]{1,0:T(8,128)(2,1)S(1)}, u32[]{:S(2)}, u32[]{:S(2)}) collective-permute-start(bf16[112,128]{1,0:T(8,128)(2,1)S(1)} %maximum_maximum_fusion), channel_id=1, source_target_pairs={{0,6},{1,7},{2,4},{3,5},{4,2},{5,3},{6,0},{7,1},{8,14},{9,15},{10,... | collective-permute-start | bytes 86024 | tf_op jit(solution)/shard_map/ppermute | solution.py:505
  7.6 3.8 %collective-permute-start.9 = (bf16[336,128]{1,0:T(8,128)(2,1)S(1)}, bf16[336,128]{1,0:T(8,128)(2,1)S(1)}, u32[]{:S(2)}, u32[]{:S(2)}) collective-permute-start(bf16[336,128]{1,0:T(8,128)(2,1)S(1)} %pad_maximum_fusion.4), channel_id=1, source_target_pairs={{0,6},{1,7},{2,4},{3,5},{4,2},{5,3},{6,0},{7,1},{8,14},{9,15},{10,... | collective-permute-start | bytes 258056 | tf_op jit(solution)/shard_map/ppermute | solution.py:505
  12.3 2.9 %collective-permute-done.1 = bf16[112,128]{1,0:T(8,128)(2,1)S(1)} collective-permute-done((bf16[112,128]{1,0:T(8,128)(2,1)S(1)}, bf16[112,128]{1,0:T(8,128)(2,1)S(1)}, u32[]{:S(2)}, u32[]{:S(2)}) %collective-permute-start.1) | collective-permute-done | bytes 28704 | tf_op jit(solution)/shard_map/ppermute | solution.py:505
  15.2 1.6 %collective-permute-start.3 = (bf16[4,112,128]{2,1,0:T(8,128)(2,1)S(1)}, bf16[4,112,128]{2,1,0:T(8,128)(2,1)S(1)}, u32[]{:S(2)}, u32[]{:S(2)}) collective-permute-start(bf16[4,112,128]{2,1,0:T(8,128)(2,1)S(1)} %pad_maximum_fusion.3), channel_id=1, source_target_pairs={{0,1},{1,0},{2,3},{3,2},{4,5},{5,4},{6,7},{7,6},{8,9},{9,8},{10,11... | collective-permute-start | bytes 344072 | tf_op jit(solution)/shard_map/ppermute | solution.py:505
  16.8 1.6 %collective-permute-done.8 = bf16[336,128]{1,0:T(8,128)(2,1)S(1)} collective-permute-done((bf16[336,128]{1,0:T(8,128)(2,1)S(1)}, bf16[336,128]{1,0:T(8,128)(2,1)S(1)}, u32[]{:S(2)}, u32[]{:S(2)}) %collective-permute-start.8) | collective-permute-done | bytes 86048 | tf_op jit(solution)/shard_map/ppermute | solution.py:505
  18.4 1.6 %collective-permute-start.14 = (bf16[4,192,128]{2,1,0:T(8,128)(2,1)S(1)}, bf16[4,192,128]{2,1,0:T(8,128)(2,1)S(1)}, u32[]{:S(2)}, u32[]{:S(2)}) collective-permute-start(bf16[4,192,128]{2,1,0:T(8,128)(2,1)S(1)} %pad_maximum_fusion.1), channel_id=1, source_target_pairs={{0,16},{1,17},{2,18},{3,19},{4,20},{5,21},{6,22},{7,23},{8,24},{9,... | collective-permute-start | bytes 589832 | tf_op jit(solution)/shard_map/ppermute | solution.py:505
  20.0 1.6 %collective-permute-start.10 = (bf16[4,144,128]{2,1,0:T(8,128)(2,1)S(1)}, bf16[4,144,128]{2,1,0:T(8,128)(2,1)S(1)}, u32[]{:S(2)}, u32[]{:S(2)}) collective-permute-start(bf16[4,144,128]{2,1,0:T(8,128)(2,1)S(1)} %pad_maximum_fusion.2), channel_id=1, source_target_pairs={{0,1},{1,0},{2,3},{3,2},{4,5},{5,4},{6,7},{7,6},{8,9},{9,8},{10,11... | collective-permute-start | bytes 442376 | tf_op jit(solution)/shard_map/ppermute | solution.py:505
  22.4 3.2 %collective-permute-done.14 = bf16[4,192,128]{2,1,0:T(8,128)(2,1)S(1)} collective-permute-done((bf16[4,192,128]{2,1,0:T(8,128)(2,1)S(1)}, bf16[4,192,128]{2,1,0:T(8,128)(2,1)S(1)}, u32[]{:S(2)}, u32[]{:S(2)}) %collective-permute-start.14) | collective-permute-done | bytes 196640 | tf_op jit(solution)/shard_map/ppermute | solution.py:505
  25.6 2.2 %collective-permute-start.15 = (bf16[8,192,128]{2,1,0:T(8,128)(2,1)S(1)}, bf16[8,192,128]{2,1,0:T(8,128)(2,1)S(1)}, u32[]{:S(2)}, u32[]{:S(2)}) collective-permute-start(bf16[8,192,128]{2,1,0:T(8,128)(2,1)S(1)} %constant_dynamic-update-slice_fusion.10.refs_4_), channel_id=1, source_target_pairs={{0,1},{1,0},{2,3},{3,2},{4,5},{5,4},{6,7},{7,6},{8,9},{9,8},{10,11... | collective-permute-start | bytes 1179656 | tf_op jit(solution)/shard_map/ppermute | solution.py:505
  31.3 4.1 %collective-permute-done.11.refs_1_ = bf16[8,144,128]{2,1,0:T(8,128)(2,1)S(1)} collective-permute-done((bf16[8,144,128]{2,1,0:T(8,128)(2,1)S(1)}, bf16[8,144,128]{2,1,0:T(8,128)(2,1)S(1)}, u32[]{:S(2)}, u32[]{:S(2)}) %collective-permute-start.11) | collective-permute-done | bytes 294944 | tf_op jit(solution)/shard_map/ppermute | solution.py:505
  35.9 4.8 %shard_map.404 = (bf16[384,1152]{1,0:T(8,128)(2,1)S(1)}, f32[1,4608]{1,0:T(1,128)S(1)}, bf16[416,1152]{1,0:T(8,128)(2,1)S(1)}, bf16[416,384]{1,0:T(8,128)(2,1)S(1)}) custom-call(s32[32]{0:T(128)S(1)} %copy-done, bf16[2,197,384]{2,1,0:T(8,128)(2,1)S(1)} %copy.48.x_ref, bf16[8,112,128]{2,1,0:T(8,128)(2,1)S(1)} %constant_dynamic-update-slice_fusion.refs_0_, ...), custom_call_target="tpu_custom_call" | custom-call | flops 5000000000 | bytes 4000000 | tf_op jit(solution)/shard_map/pallas_call | solution.py:430
  40.7 11.7 %shard_map.405 = (bf16[2,197,384]{2,1,0:T(8,128)(2,1)S(1)}, f32[416,384]{1,0:T(8,128)S(1)}, f32[1,4608]{1,0:T(1,128)S(1)}, bf16[384,384]{1,0:T(8,128)(2,1)S(1)},...) custom-call(s32[32]{0:T(128)S(1)} %copy-done, ...), custom_call_target="tpu_custom_call" | custom-call | flops 8000000000 | bytes 4000000 | tf_op jit(solution)/shard_map/pallas_call | solution.py:430
  52.5 7.7 %shard_map.406 = (bf16[2,197,384]{2,1,0:T(8,128)(2,1)S(1)}, bf16[8,112,128]{2,1,0:T(8,128)(2,1)S(1)}, bf16[8,112,128]{2,1,0:T(8,128)(2,1)S(1)}, bf16[8,112,128]{2,1,0:T(8,128)(2,1)S(1)}, bf16[8,112,128]{2,1,0:T(8,128)(2,1)S(1)}) custom-call(s32[32]{0:T(128)S(1)} %copy-done, bf16[2,197,384]{2,1,0:T(8,128)(2,1)S(1)} %copy.48.x_ref, ...), custom_call_target="tpu_custom_call" | custom-call | flops 6000000000 | bytes 4000000 | tf_op jit(solution)/shard_map/pallas_call | solution.py:430
  63.8 1.6 %collective-permute-start.20 = (bf16[8,112,128]{2,1,0:T(8,128)(2,1)S(1)}, bf16[8,112,128]{2,1,0:T(8,128)(2,1)S(1)}, u32[]{:S(2)}, u32[]{:S(2)}) collective-permute-start(bf16[8,112,128]{2,1,0:T(8,128)(2,1)S(1)} %add_convert_fusion.2), channel_id=1, source_target_pairs={{0,16},{1,17},{2,18},{3,19},{4,20},{5,21},{6,22},{7,23},{8,24},{9,... | collective-permute-start | bytes 688136 | tf_op jit(solution)/shard_map/ppermute | solution.py:505
  65.4 1.6 %collective-permute-start.31 = (bf16[8,144,128]{2,1,0:T(8,128)(2,1)S(1)}, bf16[8,144,128]{2,1,0:T(8,128)(2,1)S(1)}, u32[]{:S(2)}, u32[]{:S(2)}) collective-permute-start(bf16[8,144,128]{2,1,0:T(8,128)(2,1)S(1)} %add_convert_fusion.1), channel_id=1, source_target_pairs={{0,1},{1,0},{2,3},{3,2},{4,5},{5,4},{6,7},{7,6},{8,9},{9,8},{10,11... | collective-permute-start | bytes 884744 | tf_op jit(solution)/shard_map/ppermute | solution.py:505
  67.0 4.4 %collective-permute-done.20 = bf16[8,112,128]{2,1,0:T(8,128)(2,1)S(1)} collective-permute-done((bf16[8,112,128]{2,1,0:T(8,128)(2,1)S(1)}, bf16[8,112,128]{2,1,0:T(8,128)(2,1)S(1)}, u32[]{:S(2)}, u32[]{:S(2)}) %collective-permute-start.20) | collective-permute-done | bytes 229408 | tf_op jit(solution)/shard_map/ppermute | solution.py:505
  71.5 1.6 %collective-permute-start.21 = (bf16[4,112,128]{2,1,0:T(8,128)(2,1)S(1)}, bf16[4,112,128]{2,1,0:T(8,128)(2,1)S(1)}, u32[]{:S(2)}, u32[]{:S(2)}) collective-permute-start(bf16[4,112,128]{2,1,0:T(8,128)(2,1)S(1)} %slice.202), channel_id=1, source_target_pairs={{0,1},{1,0},{2,3},{3,2},{4,5},{5,4},{6,7},{7,6},{8,9},{9,8},{10,11... | collective-permute-start | bytes 344072 | tf_op jit(solution)/shard_map/ppermute | solution.py:505
  74.8 1.9 %collective-permute-done.21 = bf16[4,112,128]{2,1,0:T(8,128)(2,1)S(1)} collective-permute-done((bf16[4,112,128]{2,1,0:T(8,128)(2,1)S(1)}, bf16[4,112,128]{2,1,0:T(8,128)(2,1)S(1)}, u32[]{:S(2)}, u32[]{:S(2)}) %collective-permute-start.21) | collective-permute-done | bytes 114720 | tf_op jit(solution)/shard_map/ppermute | solution.py:505
  76.8 1.7 %collective-permute-start.24 = (bf16[112,128]{1,0:T(8,128)(2,1)S(1)}, bf16[112,128]{1,0:T(8,128)(2,1)S(1)}, u32[]{:S(2)}, u32[]{:S(2)}) collective-permute-start(bf16[112,128]{1,0:T(8,128)(2,1)S(1)} %get-tuple-element.130), channel_id=1, source_target_pairs={{0,6},{1,7},{2,4},{3,5},{4,2},{5,3},{6,0},{7,1},{8,14},{9,15},{10,... | collective-permute-start | bytes 86024 | tf_op jit(solution)/shard_map/ppermute | solution.py:505
  78.6 1.7 %collective-permute-start.23 = (bf16[112,128]{1,0:T(8,128)(2,1)S(1)}, bf16[112,128]{1,0:T(8,128)(2,1)S(1)}, u32[]{:S(2)}, u32[]{:S(2)}) collective-permute-start(bf16[112,128]{1,0:T(8,128)(2,1)S(1)} %get-tuple-element.131), channel_id=1, source_target_pairs={{0,4},{1,5},{2,6},{3,7},{4,0},{5,1},{6,2},{7,3},{8,12},{9,13},{10,... | collective-permute-start | bytes 86024 | tf_op jit(solution)/shard_map/ppermute | solution.py:505
  87.0 4.2 %collective-permute-done.28 = bf16[4,192,128]{2,1,0:T(8,128)(2,1)S(1)} collective-permute-done((bf16[4,192,128]{2,1,0:T(8,128)(2,1)S(1)}, bf16[4,192,128]{2,1,0:T(8,128)(2,1)S(1)}, u32[]{:S(2)}, u32[]{:S(2)}) %collective-permute-start.28) | collective-permute-done | bytes 196640 | tf_op jit(solution)/shard_map/ppermute | solution.py:505
  92.2 2.3 %collective-permute-start.35 = (bf16[336,128]{1,0:T(8,128)(2,1)S(1)}, bf16[336,128]{1,0:T(8,128)(2,1)S(1)}, u32[]{:S(2)}, u32[]{:S(2)}) collective-permute-start(bf16[336,128]{1,0:T(8,128)(2,1)S(1)} %get-tuple-element.123), channel_id=1, source_target_pairs={{0,6},{1,7},{2,4},{3,5},{4,2},{5,3},{6,0},{7,1},{8,14},{9,15},{10,... | collective-permute-start | bytes 258056 | tf_op jit(solution)/shard_map/ppermute | solution.py:505
  96.5 2.0 %collective-permute-done.35 = bf16[336,128]{1,0:T(8,128)(2,1)S(1)} collective-permute-done((bf16[336,128]{1,0:T(8,128)(2,1)S(1)}, bf16[336,128]{1,0:T(8,128)(2,1)S(1)}, u32[]{:S(2)}, u32[]{:S(2)}) %collective-permute-start.35) | collective-permute-done | bytes 86048 | tf_op jit(solution)/shard_map/ppermute | solution.py:505
  98.5 1.9 %collective-permute-done.34 = bf16[336,128]{1,0:T(8,128)(2,1)S(1)} collective-permute-done((bf16[336,128]{1,0:T(8,128)(2,1)S(1)}, bf16[336,128]{1,0:T(8,128)(2,1)S(1)}, u32[]{:S(2)}, u32[]{:S(2)}) %collective-permute-start.34) | collective-permute-done | bytes 86048 | tf_op jit(solution)/shard_map/ppermute | solution.py:505
  (154 shorter events, 24.2 us)
Async XLA Ops:
  1.8 9.8 %collective-permute-start.2 = (bf16[112,128]{1,0:T(8,128)(2,1)S(1)}, bf16[112,128]{1,0:T(8,128)(2,1)S(1)}, u32[]{:S(2)}, u32[]{:S(2)}) collective-permute-start(bf16[112,128]{1,0:T(8,128)(2,1)S(1)} %maximum_maximum_fusion), channel_id=1, source_target_pairs={{0,6},{1,7},{2,4},{3,5},{4,2},{5,3},{6,0},{7,1},{8,14},{9,15},{10,... | collective-permute-start | bytes 86024 | tf_op jit(solution)/shard_map/ppermute | solution.py:505
  6.9 8.2 %collective-permute-start.1 = (bf16[112,128]{1,0:T(8,128)(2,1)S(1)}, bf16[112,128]{1,0:T(8,128)(2,1)S(1)}, u32[]{:S(2)}, u32[]{:S(2)}) collective-permute-start(bf16[112,128]{1,0:T(8,128)(2,1)S(1)} %maximum_maximum_fusion), channel_id=1, source_target_pairs={{0,4},{1,5},{2,6},{3,7},{4,0},{5,1},{6,2},{7,3},{8,12},{9,13},{10,... | collective-permute-start | bytes 86024 | tf_op jit(solution)/shard_map/ppermute | solution.py:505
  6.9 8.2 %collective-permute-start = (bf16[112,128]{1,0:T(8,128)(2,1)S(1)}, bf16[112,128]{1,0:T(8,128)(2,1)S(1)}, u32[]{:S(2)}, u32[]{:S(2)}) collective-permute-start(bf16[112,128]{1,0:T(8,128)(2,1)S(1)} %maximum_maximum_fusion), channel_id=1, source_target_pairs={{0,2},{1,3},{2,0},{3,1},{4,6},{5,7},{6,4},{7,5},{8,10},{9,11},{10,... | collective-permute-start | bytes 86024 | tf_op jit(solution)/shard_map/ppermute | solution.py:505
  7.6 9.1 %collective-permute-start.9 = (bf16[336,128]{1,0:T(8,128)(2,1)S(1)}, bf16[336,128]{1,0:T(8,128)(2,1)S(1)}, u32[]{:S(2)}, u32[]{:S(2)}) collective-permute-start(bf16[336,128]{1,0:T(8,128)(2,1)S(1)} %pad_maximum_fusion.4), channel_id=1, source_target_pairs={{0,6},{1,7},{2,4},{3,5},{4,2},{5,3},{6,0},{7,1},{8,14},{9,15},{10,... | collective-permute-start | bytes 258056 | tf_op jit(solution)/shard_map/ppermute | solution.py:505
  11.5 6.9 %collective-permute-start.8 = (bf16[336,128]{1,0:T(8,128)(2,1)S(1)}, bf16[336,128]{1,0:T(8,128)(2,1)S(1)}, u32[]{:S(2)}, u32[]{:S(2)}) collective-permute-start(bf16[336,128]{1,0:T(8,128)(2,1)S(1)} %pad_maximum_fusion.4), channel_id=1, source_target_pairs={{0,4},{1,5},{2,6},{3,7},{4,0},{5,1},{6,2},{7,3},{8,12},{9,13},{10,... | collective-permute-start | bytes 258056 | tf_op jit(solution)/shard_map/ppermute | solution.py:505
  11.6 6.8 %collective-permute-start.7 = (bf16[336,128]{1,0:T(8,128)(2,1)S(1)}, bf16[336,128]{1,0:T(8,128)(2,1)S(1)}, u32[]{:S(2)}, u32[]{:S(2)}) collective-permute-start(bf16[336,128]{1,0:T(8,128)(2,1)S(1)} %pad_maximum_fusion.4), channel_id=1, source_target_pairs={{0,2},{1,3},{2,0},{3,1},{4,6},{5,7},{6,4},{7,5},{8,10},{9,11},{10,... | collective-permute-start | bytes 258056 | tf_op jit(solution)/shard_map/ppermute | solution.py:505
  15.2 6.6 %collective-permute-start.3 = (bf16[4,112,128]{2,1,0:T(8,128)(2,1)S(1)}, bf16[4,112,128]{2,1,0:T(8,128)(2,1)S(1)}, u32[]{:S(2)}, u32[]{:S(2)}) collective-permute-start(bf16[4,112,128]{2,1,0:T(8,128)(2,1)S(1)} %pad_maximum_fusion.3), channel_id=1, source_target_pairs={{0,1},{1,0},{2,3},{3,2},{4,5},{5,4},{6,7},{7,6},{8,9},{9,8},{10,11... | collective-permute-start | bytes 344072 | tf_op jit(solution)/shard_map/ppermute | solution.py:505
  18.4 7.2 %collective-permute-start.14 = (bf16[4,192,128]{2,1,0:T(8,128)(2,1)S(1)}, bf16[4,192,128]{2,1,0:T(8,128)(2,1)S(1)}, u32[]{:S(2)}, u32[]{:S(2)}) collective-permute-start(bf16[4,192,128]{2,1,0:T(8,128)(2,1)S(1)} %pad_maximum_fusion.1), channel_id=1, source_target_pairs={{0,16},{1,17},{2,18},{3,19},{4,20},{5,21},{6,22},{7,23},{8,24},{9,... | collective-permute-start | bytes 589832 | tf_op jit(solution)/shard_map/ppermute | solution.py:505
  20.0 7.8 %collective-permute-start.10 = (bf16[4,144,128]{2,1,0:T(8,128)(2,1)S(1)}, bf16[4,144,128]{2,1,0:T(8,128)(2,1)S(1)}, u32[]{:S(2)}, u32[]{:S(2)}) collective-permute-start(bf16[4,144,128]{2,1,0:T(8,128)(2,1)S(1)} %pad_maximum_fusion.2), channel_id=1, source_target_pairs={{0,1},{1,0},{2,3},{3,2},{4,5},{5,4},{6,7},{7,6},{8,9},{9,8},{10,11... | collective-permute-start | bytes 442376 | tf_op jit(solution)/shard_map/ppermute | solution.py:505
  21.8 8.8 %collective-permute-start.4 = (bf16[8,112,128]{2,1,0:T(8,128)(2,1)S(1)}, bf16[8,112,128]{2,1,0:T(8,128)(2,1)S(1)}, u32[]{:S(2)}, u32[]{:S(2)}) collective-permute-start(bf16[8,112,128]{2,1,0:T(8,128)(2,1)S(1)} %constant_dynamic-update-slice_fusion.refs_0_), channel_id=1, source_target_pairs={{0,16},{1,17},{2,18},{3,19},{4,20},{5,21},{6,22},{7,23},{8,24},{9,... | collective-permute-start | bytes 688136 | tf_op jit(solution)/shard_map/ppermute | solution.py:505
  25.6 9.8 %collective-permute-start.15 = (bf16[8,192,128]{2,1,0:T(8,128)(2,1)S(1)}, bf16[8,192,128]{2,1,0:T(8,128)(2,1)S(1)}, u32[]{:S(2)}, u32[]{:S(2)}) collective-permute-start(bf16[8,192,128]{2,1,0:T(8,128)(2,1)S(1)} %constant_dynamic-update-slice_fusion.10.refs_4_), channel_id=1, source_target_pairs={{0,1},{1,0},{2,3},{3,2},{4,5},{5,4},{6,7},{7,6},{8,9},{9,8},{10,11... | collective-permute-start | bytes 1179656 | tf_op jit(solution)/shard_map/ppermute | solution.py:505
  27.9 7.5 %collective-permute-start.11 = (bf16[8,144,128]{2,1,0:T(8,128)(2,1)S(1)}, bf16[8,144,128]{2,1,0:T(8,128)(2,1)S(1)}, u32[]{:S(2)}, u32[]{:S(2)}) collective-permute-start(bf16[8,144,128]{2,1,0:T(8,128)(2,1)S(1)} %constant_dynamic-update-slice_fusion.5.refs_0_), channel_id=1, source_target_pairs={{0,16},{1,17},{2,18},{3,19},{4,20},{5,21},{6,22},{7,23},{8,24},{9,... | collective-permute-start | bytes 884744 | tf_op jit(solution)/shard_map/ppermute | solution.py:505
  30.6 10.1 %collective-permute-start.12 = (bf16[8,144,128]{2,1,0:T(8,128)(2,1)S(1)}, bf16[8,144,128]{2,1,0:T(8,128)(2,1)S(1)}, u32[]{:S(2)}, u32[]{:S(2)}) collective-permute-start(bf16[8,144,128]{2,1,0:T(8,128)(2,1)S(1)} %constant_dynamic-update-slice_fusion.5.refs_0_), channel_id=1, source_target_pairs={{0,8},{1,9},{2,10},{3,11},{4,12},{5,13},{6,14},{7,15},{8,0},{9,1},... | collective-permute-start | bytes 884744 | tf_op jit(solution)/shard_map/ppermute | solution.py:505
  31.2 9.5 %collective-permute-start.16 = (bf16[8,192,128]{2,1,0:T(8,128)(2,1)S(1)}, bf16[8,192,128]{2,1,0:T(8,128)(2,1)S(1)}, u32[]{:S(2)}, u32[]{:S(2)}) collective-permute-start(bf16[8,192,128]{2,1,0:T(8,128)(2,1)S(1)} %constant_dynamic-update-slice_fusion.10.refs_4_), channel_id=1, source_target_pairs={{0,8},{1,9},{2,10},{3,11},{4,12},{5,13},{6,14},{7,15},{8,0},{9,1},... | collective-permute-start | bytes 1179656 | tf_op jit(solution)/shard_map/ppermute | solution.py:505
  62.7 14.1 %collective-permute-start.29 = (bf16[8,144,128]{2,1,0:T(8,128)(2,1)S(1)}, bf16[8,144,128]{2,1,0:T(8,128)(2,1)S(1)}, u32[]{:S(2)}, u32[]{:S(2)}) collective-permute-start(bf16[8,144,128]{2,1,0:T(8,128)(2,1)S(1)} %get-tuple-element.65), channel_id=1, source_target_pairs={{0,8},{1,9},{2,10},{3,11},{4,12},{5,13},{6,14},{7,15},{8,0},{9,1},... | collective-permute-start | bytes 884744 | tf_op jit(solution)/shard_map/ppermute | solution.py:505
  63.2 22.1 %collective-permute-start.25 = (bf16[8,192,128]{2,1,0:T(8,128)(2,1)S(1)}, bf16[8,192,128]{2,1,0:T(8,128)(2,1)S(1)}, u32[]{:S(2)}, u32[]{:S(2)}) collective-permute-start(bf16[8,192,128]{2,1,0:T(8,128)(2,1)S(1)} %get-tuple-element.61), channel_id=1, source_target_pairs={{0,8},{1,9},{2,10},{3,11},{4,12},{5,13},{6,14},{7,15},{8,0},{9,1},... | collective-permute-start | bytes 1179656 | tf_op jit(solution)/shard_map/ppermute | solution.py:505
  63.3 9.9 %collective-permute-start.26 = (bf16[8,192,128]{2,1,0:T(8,128)(2,1)S(1)}, bf16[8,192,128]{2,1,0:T(8,128)(2,1)S(1)}, u32[]{:S(2)}, u32[]{:S(2)}) collective-permute-start(bf16[8,192,128]{2,1,0:T(8,128)(2,1)S(1)} %get-tuple-element.63), channel_id=1, source_target_pairs={{0,8},{1,9},{2,10},{3,11},{4,12},{5,13},{6,14},{7,15},{8,0},{9,1},... | collective-permute-start | bytes 1179656 | tf_op jit(solution)/shard_map/ppermute | solution.py:505
  63.8 7.7 %collective-permute-start.20 = (bf16[8,112,128]{2,1,0:T(8,128)(2,1)S(1)}, bf16[8,112,128]{2,1,0:T(8,128)(2,1)S(1)}, u32[]{:S(2)}, u32[]{:S(2)}) collective-permute-start(bf16[8,112,128]{2,1,0:T(8,128)(2,1)S(1)} %add_convert_fusion.2), channel_id=1, source_target_pairs={{0,16},{1,17},{2,18},{3,19},{4,20},{5,21},{6,22},{7,23},{8,24},{9,... | collective-permute-start | bytes 688136 | tf_op jit(solution)/shard_map/ppermute | solution.py:505
  65.4 13.1 %collective-permute-start.31 = (bf16[8,144,128]{2,1,0:T(8,128)(2,1)S(1)}, bf16[8,144,128]{2,1,0:T(8,128)(2,1)S(1)}, u32[]{:S(2)}, u32[]{:S(2)}) collective-permute-start(bf16[8,144,128]{2,1,0:T(8,128)(2,1)S(1)} %add_convert_fusion.1), channel_id=1, source_target_pairs={{0,1},{1,0},{2,3},{3,2},{4,5},{5,4},{6,7},{7,6},{8,9},{9,8},{10,11... | collective-permute-start | bytes 884744 | tf_op jit(solution)/shard_map/ppermute | solution.py:505
  73.2 12.0 %collective-permute-start.27 = (bf16[8,192,128]{2,1,0:T(8,128)(2,1)S(1)}, bf16[8,192,128]{2,1,0:T(8,128)(2,1)S(1)}, u32[]{:S(2)}, u32[]{:S(2)}) collective-permute-start(bf16[8,192,128]{2,1,0:T(8,128)(2,1)S(1)} %add_convert_fusion), channel_id=1, source_target_pairs={{0,16},{1,17},{2,18},{3,19},{4,20},{5,21},{6,22},{7,23},{8,24},{9,... | collective-permute-start | bytes 1179656 | tf_op jit(solution)/shard_map/ppermute | solution.py:505
  81.1 5.8 %collective-permute-start.32 = (bf16[4,144,128]{2,1,0:T(8,128)(2,1)S(1)}, bf16[4,144,128]{2,1,0:T(8,128)(2,1)S(1)}, u32[]{:S(2)}, u32[]{:S(2)}) collective-permute-start(bf16[4,144,128]{2,1,0:T(8,128)(2,1)S(1)} %slice.201), channel_id=1, source_target_pairs={{0,16},{1,17},{2,18},{3,19},{4,20},{5,21},{6,22},{7,23},{8,24},{9,... | collective-permute-start | bytes 442376 | tf_op jit(solution)/shard_map/ppermute | solution.py:505
  85.4 5.7 %collective-permute-start.28 = (bf16[4,192,128]{2,1,0:T(8,128)(2,1)S(1)}, bf16[4,192,128]{2,1,0:T(8,128)(2,1)S(1)}, u32[]{:S(2)}, u32[]{:S(2)}) collective-permute-start(bf16[4,192,128]{2,1,0:T(8,128)(2,1)S(1)} %slice.200), channel_id=1, source_target_pairs={{0,1},{1,0},{2,3},{3,2},{4,5},{5,4},{6,7},{7,6},{8,9},{9,8},{10,11... | collective-permute-start | bytes 589832 | tf_op jit(solution)/shard_map/ppermute | solution.py:505
  92.2 6.3 %collective-permute-start.35 = (bf16[336,128]{1,0:T(8,128)(2,1)S(1)}, bf16[336,128]{1,0:T(8,128)(2,1)S(1)}, u32[]{:S(2)}, u32[]{:S(2)}) collective-permute-start(bf16[336,128]{1,0:T(8,128)(2,1)S(1)} %get-tuple-element.123), channel_id=1, source_target_pairs={{0,6},{1,7},{2,4},{3,5},{4,2},{5,3},{6,0},{7,1},{8,14},{9,15},{10,... | collective-permute-start | bytes 258056 | tf_op jit(solution)/shard_map/ppermute | solution.py:505
  94.5 5.8 %collective-permute-start.34 = (bf16[336,128]{1,0:T(8,128)(2,1)S(1)}, bf16[336,128]{1,0:T(8,128)(2,1)S(1)}, u32[]{:S(2)}, u32[]{:S(2)}) collective-permute-start(bf16[336,128]{1,0:T(8,128)(2,1)S(1)} %get-tuple-element.124), channel_id=1, source_target_pairs={{0,4},{1,5},{2,6},{3,7},{4,0},{5,1},{6,2},{7,3},{8,12},{9,13},{10,... | collective-permute-start | bytes 258056 | tf_op jit(solution)/shard_map/ppermute | solution.py:505
  (33 other events, 114.8 us)

commit v3 on v2

--- a/solution.py
+++ b/solution.py
@@ -5,6 +5,7 @@
 import jax.numpy as jnp
 from jax import lax
 from jax.experimental import pallas as pl
+from jax.experimental.layout import Layout, with_layout_constraint
 from jax.experimental.pallas import tpu as pltpu
 from jax.sharding import PartitionSpec as P
 
@@ -55,6 +56,7 @@
 BIAS_PART = BIASES // BLOCKS
 CHUNKS = FF // D
 Y_BIT, Z_LOW, Z_HIGH, CORE_BIT, X_BIT = 1, 2, 4, 8, 16
+TOKEN_MAJOR = Layout(major_to_minor=(1, 0, 2))
 LINE = (Z_LOW, Z_HIGH, Z_LOW + Z_HIGH)
 
 
@@ -555,7 +557,7 @@
     return pieces
 
 
-def reduce_blocks(pieces):
+def reduce_blocks(pieces, ready):
     done = []
     for color, (near, far) in enumerate(((Y_BIT, X_BIT), (X_BIT, Y_BIT))):
         keep, keep_far, send, send_far = pieces[4 * color : 4 * color + 4]
@@ -565,9 +567,12 @@
         from_core = exchange(send, CORE_BIT)
         plane = keep.astype(F32) + from_core.astype(F32) + crossed.astype(F32)
         crossed = exchange(plane[4:].astype(BF16), near)
+        if color == 1:
+            ready = [with_layout_constraint(value, TOKEN_MAJOR) for value in ready]
+            crossed, *ready = lax.optimization_barrier((crossed, *ready))
         done.append(plane[:4] + crossed.astype(F32))
     line = jnp.concatenate(done, axis=1)
-    return sum_line(line)
+    return sum_line(line), ready
 
 
 def ordered_pieces(whole, split):
@@ -663,7 +668,7 @@
         swaps, counts, images, qkv, grad_mid, w_qkv, w_out, vec, vec_grad
     )
     if swaps:
-        second_sum = reduce_blocks(second_grads)
+        second_sum, (block_out, images_grad) = reduce_blocks(second_grads, (block_out, images_grad))
         first_sum = reduce_line(first_grads)
         owned = split_blocks(first_sum, second_sum)
     else:

time: 102 us -> 103 us (level)
    pallas_call x0 -> x2, local copies, waits for them, and re-layouts: none -> 1.9 us  [call(): pl.pallas_call(functools.partial(kernel, swaps), out_shape=outs, in_specs...]
    unnamed x55 -> x53, local copies, waits for them, and re-layouts: 3.07 us -> 1.4 us
  transfers between devices with their start and end apart: 36 -> 36, of which waited for: 14 -> 15; matrix products, arithmetic and copies ran while one was open for 5% -> 5% of each run, Pallas kernels for 5% -> 5%
where the time goes in v3:
time: 103 us
  starting transfers between devices  37.8 us (37%)
  waiting for transfers between devices  31.2 us (30%)
  Pallas kernels  24.2 us (23%)
  other arithmetic  5.14 us (5%)
  local copies, waits for them, and re-layouts  3.57 us (3%)
  between operations  1.2 us (1%)
    ppermute x36, starting transfers between devices, exchange(): return lax.ppermute(value, AXES, [(i, i ^ mask) for i in range(BLOCKS)])  37.8 us
    ppermute x36, waiting for transfers between devices, exchange(): return lax.ppermute(value, AXES, [(i, i ^ mask) for i in range(BLOCKS)])  31.2 us
    pallas_call x3, Pallas kernels, call(): pl.pallas_call(functools.partial(kernel, swaps), out_shape=outs, in_specs...  24.2 us
    sub x5, other arithmetic, adam_update(): return (weight - step_rate * change, first_new, second_new)  3.23 us
  transfers between devices with their start and end apart: 36, of which 15 were waited for; matrix products, arithmetic and copies ran while one was open for 5% of the time, Pallas kernels for 5%

profile of v3, /device:TPU:0, one launch (start us, length us, event | category | flops | bytes accessed | tf_op | source)
XLA Modules:
  0.0 103.1 jit_solution(2862844858446536389)
XLA Ops:
  1.8 5.1 %collective-permute-start.2 = (bf16[112,128]{1,0:T(8,128)(2,1)S(1)}, bf16[112,128]{1,0:T(8,128)(2,1)S(1)}, u32[]{:S(2)}, u32[]{:S(2)}) collective-permute-start(bf16[112,128]{1,0:T(8,128)(2,1)S(1)} %maximum_maximum_fusion), channel_id=1, source_target_pairs={{0,6},{1,7},{2,4},{3,5},{4,2},{5,3},{6,0},{7,1},{8,14},{9,15},{10,... | collective-permute-start | bytes 86024 | tf_op jit(solution)/shard_map/ppermute | solution.py:507
  7.6 3.8 %collective-permute-start.9 = (bf16[336,128]{1,0:T(8,128)(2,1)S(1)}, bf16[336,128]{1,0:T(8,128)(2,1)S(1)}, u32[]{:S(2)}, u32[]{:S(2)}) collective-permute-start(bf16[336,128]{1,0:T(8,128)(2,1)S(1)} %pad_maximum_fusion.4), channel_id=1, source_target_pairs={{0,6},{1,7},{2,4},{3,5},{4,2},{5,3},{6,0},{7,1},{8,14},{9,15},{10,... | collective-permute-start | bytes 258056 | tf_op jit(solution)/shard_map/ppermute | solution.py:507
  12.3 2.9 %collective-permute-done.1 = bf16[112,128]{1,0:T(8,128)(2,1)S(1)} collective-permute-done((bf16[112,128]{1,0:T(8,128)(2,1)S(1)}, bf16[112,128]{1,0:T(8,128)(2,1)S(1)}, u32[]{:S(2)}, u32[]{:S(2)}) %collective-permute-start.1) | collective-permute-done | bytes 28704 | tf_op jit(solution)/shard_map/ppermute | solution.py:507
  15.2 1.6 %collective-permute-start.3 = (bf16[4,112,128]{2,1,0:T(8,128)(2,1)S(1)}, bf16[4,112,128]{2,1,0:T(8,128)(2,1)S(1)}, u32[]{:S(2)}, u32[]{:S(2)}) collective-permute-start(bf16[4,112,128]{2,1,0:T(8,128)(2,1)S(1)} %pad_maximum_fusion.3), channel_id=1, source_target_pairs={{0,1},{1,0},{2,3},{3,2},{4,5},{5,4},{6,7},{7,6},{8,9},{9,8},{10,11... | collective-permute-start | bytes 344072 | tf_op jit(solution)/shard_map/ppermute | solution.py:507
  16.8 1.6 %collective-permute-done.8 = bf16[336,128]{1,0:T(8,128)(2,1)S(1)} collective-permute-done((bf16[336,128]{1,0:T(8,128)(2,1)S(1)}, bf16[336,128]{1,0:T(8,128)(2,1)S(1)}, u32[]{:S(2)}, u32[]{:S(2)}) %collective-permute-start.8) | collective-permute-done | bytes 86048 | tf_op jit(solution)/shard_map/ppermute | solution.py:507
  18.4 1.6 %collective-permute-start.14 = (bf16[4,192,128]{2,1,0:T(8,128)(2,1)S(1)}, bf16[4,192,128]{2,1,0:T(8,128)(2,1)S(1)}, u32[]{:S(2)}, u32[]{:S(2)}) collective-permute-start(bf16[4,192,128]{2,1,0:T(8,128)(2,1)S(1)} %pad_maximum_fusion.1), channel_id=1, source_target_pairs={{0,16},{1,17},{2,18},{3,19},{4,20},{5,21},{6,22},{7,23},{8,24},{9,... | collective-permute-start | bytes 589832 | tf_op jit(solution)/shard_map/ppermute | solution.py:507
  20.0 1.6 %collective-permute-start.10 = (bf16[4,144,128]{2,1,0:T(8,128)(2,1)S(1)}, bf16[4,144,128]{2,1,0:T(8,128)(2,1)S(1)}, u32[]{:S(2)}, u32[]{:S(2)}) collective-permute-start(bf16[4,144,128]{2,1,0:T(8,128)(2,1)S(1)} %pad_maximum_fusion.2), channel_id=1, source_target_pairs={{0,1},{1,0},{2,3},{3,2},{4,5},{5,4},{6,7},{7,6},{8,9},{9,8},{10,11... | collective-permute-start | bytes 442376 | tf_op jit(solution)/shard_map/ppermute | solution.py:507
  22.4 3.2 %collective-permute-done.14 = bf16[4,192,128]{2,1,0:T(8,128)(2,1)S(1)} collective-permute-done((bf16[4,192,128]{2,1,0:T(8,128)(2,1)S(1)}, bf16[4,192,128]{2,1,0:T(8,128)(2,1)S(1)}, u32[]{:S(2)}, u32[]{:S(2)}) %collective-permute-start.14) | collective-permute-done | bytes 196640 | tf_op jit(solution)/shard_map/ppermute | solution.py:507
  25.6 2.2 %collective-permute-start.15 = (bf16[8,192,128]{2,1,0:T(8,128)(2,1)S(1)}, bf16[8,192,128]{2,1,0:T(8,128)(2,1)S(1)}, u32[]{:S(2)}, u32[]{:S(2)}) collective-permute-start(bf16[8,192,128]{2,1,0:T(8,128)(2,1)S(1)} %constant_dynamic-update-slice_fusion.10.refs_4_), channel_id=1, source_target_pairs={{0,1},{1,0},{2,3},{3,2},{4,5},{5,4},{6,7},{7,6},{8,9},{9,8},{10,11... | collective-permute-start | bytes 1179656 | tf_op jit(solution)/shard_map/ppermute | solution.py:507
  27.9 1.6 %collective-permute-start.11 = (bf16[8,144,128]{2,1,0:T(8,128)(2,1)S(1)}, bf16[8,144,128]{2,1,0:T(8,128)(2,1)S(1)}, u32[]{:S(2)}, u32[]{:S(2)}) collective-permute-start(bf16[8,144,128]{2,1,0:T(8,128)(2,1)S(1)} %constant_dynamic-update-slice_fusion.5.refs_0_), channel_id=1, source_target_pairs={{0,16},{1,17},{2,18},{3,19},{4,20},{5,21},{6,22},{7,23},{8,24},{9,... | collective-permute-start | bytes 884744 | tf_op jit(solution)/shard_map/ppermute | solution.py:507
  31.3 4.1 %collective-permute-done.11.refs_1_ = bf16[8,144,128]{2,1,0:T(8,128)(2,1)S(1)} collective-permute-done((bf16[8,144,128]{2,1,0:T(8,128)(2,1)S(1)}, bf16[8,144,128]{2,1,0:T(8,128)(2,1)S(1)}, u32[]{:S(2)}, u32[]{:S(2)}) %collective-permute-start.11) | collective-permute-done | bytes 294944 | tf_op jit(solution)/shard_map/ppermute | solution.py:507
  35.9 4.8 %shard_map.404 = (bf16[384,1152]{1,0:T(8,128)(2,1)S(1)}, f32[1,4608]{1,0:T(1,128)S(1)}, bf16[416,1152]{1,0:T(8,128)(2,1)S(1)}, bf16[416,384]{1,0:T(8,128)(2,1)S(1)}) custom-call(s32[32]{0:T(128)S(1)} %copy-done, bf16[2,197,384]{2,1,0:T(8,128)(2,1)S(1)} %copy.48.x_ref, bf16[8,112,128]{2,1,0:T(8,128)(2,1)S(1)} %constant_dynamic-update-slice_fusion.refs_0_, ...), custom_call_target="tpu_custom_call" | custom-call | flops 5000000000 | bytes 4000000 | tf_op jit(solution)/shard_map/pallas_call | solution.py:432
  40.7 11.7 %shard_map.405 = (bf16[2,197,384]{2,1,0:T(8,128)(2,1)S(1)}, f32[416,384]{1,0:T(8,128)S(1)}, f32[1,4608]{1,0:T(1,128)S(1)}, bf16[384,384]{1,0:T(8,128)(2,1)S(1)},...) custom-call(s32[32]{0:T(128)S(1)} %copy-done, ...), custom_call_target="tpu_custom_call" | custom-call | flops 8000000000 | bytes 4000000 | tf_op jit(solution)/shard_map/pallas_call | solution.py:432
  52.5 7.7 %shard_map.406 = (bf16[2,197,384]{2,1,0:T(8,128)(2,1)S(1)}, bf16[8,112,128]{2,1,0:T(8,128)(2,1)S(1)}, bf16[8,112,128]{2,1,0:T(8,128)(2,1)S(1)}, bf16[8,112,128]{2,1,0:T(8,128)(2,1)S(1)}, bf16[8,112,128]{2,1,0:T(8,128)(2,1)S(1)}) custom-call(s32[32]{0:T(128)S(1)} %copy-done, bf16[2,197,384]{2,1,0:T(8,128)(2,1)S(1)} %copy.48.x_ref, ...), custom_call_target="tpu_custom_call" | custom-call | flops 6000000000 | bytes 4000000 | tf_op jit(solution)/shard_map/pallas_call | solution.py:432
  63.8 1.6 %collective-permute-start.24 = (bf16[8,112,128]{2,1,0:T(8,128)(2,1)S(1)}, bf16[8,112,128]{2,1,0:T(8,128)(2,1)S(1)}, u32[]{:S(2)}, u32[]{:S(2)}) collective-permute-start(bf16[8,112,128]{2,1,0:T(8,128)(2,1)S(1)} %add_convert_fusion.2), channel_id=1, source_target_pairs={{0,16},{1,17},{2,18},{3,19},{4,20},{5,21},{6,22},{7,23},{8,24},{9,... | collective-permute-start | bytes 688136 | tf_op jit(solution)/shard_map/ppermute | solution.py:507
  65.4 1.6 %collective-permute-start.20 = (bf16[8,144,128]{2,1,0:T(8,128)(2,1)S(1)}, bf16[8,144,128]{2,1,0:T(8,128)(2,1)S(1)}, u32[]{:S(2)}, u32[]{:S(2)}) collective-permute-start(bf16[8,144,128]{2,1,0:T(8,128)(2,1)S(1)} %add_convert_fusion.1), channel_id=1, source_target_pairs={{0,1},{1,0},{2,3},{3,2},{4,5},{5,4},{6,7},{7,6},{8,9},{9,8},{10,11... | collective-permute-start | bytes 884744 | tf_op jit(solution)/shard_map/ppermute | solution.py:507
  67.0 4.4 %collective-permute-done.24 = bf16[8,112,128]{2,1,0:T(8,128)(2,1)S(1)} collective-permute-done((bf16[8,112,128]{2,1,0:T(8,128)(2,1)S(1)}, bf16[8,112,128]{2,1,0:T(8,128)(2,1)S(1)}, u32[]{:S(2)}, u32[]{:S(2)}) %collective-permute-start.24) | collective-permute-done | bytes 229408 | tf_op jit(solution)/shard_map/ppermute | solution.py:507
  71.5 1.6 %collective-permute-start.25 = (bf16[4,112,128]{2,1,0:T(8,128)(2,1)S(1)}, bf16[4,112,128]{2,1,0:T(8,128)(2,1)S(1)}, u32[]{:S(2)}, u32[]{:S(2)}) collective-permute-start(bf16[4,112,128]{2,1,0:T(8,128)(2,1)S(1)} %slice.202), channel_id=1, source_target_pairs={{0,1},{1,0},{2,3},{3,2},{4,5},{5,4},{6,7},{7,6},{8,9},{9,8},{10,11... | collective-permute-start | bytes 344072 | tf_op jit(solution)/shard_map/ppermute | solution.py:507
  74.8 1.9 %collective-permute-done.25 = bf16[4,112,128]{2,1,0:T(8,128)(2,1)S(1)} collective-permute-done((bf16[4,112,128]{2,1,0:T(8,128)(2,1)S(1)}, bf16[4,112,128]{2,1,0:T(8,128)(2,1)S(1)}, u32[]{:S(2)}, u32[]{:S(2)}) %collective-permute-start.25) | collective-permute-done | bytes 114720 | tf_op jit(solution)/shard_map/ppermute | solution.py:507
  76.8 1.7 %collective-permute-start.28 = (bf16[112,128]{1,0:T(8,128)(2,1)S(1)}, bf16[112,128]{1,0:T(8,128)(2,1)S(1)}, u32[]{:S(2)}, u32[]{:S(2)}) collective-permute-start(bf16[112,128]{1,0:T(8,128)(2,1)S(1)} %get-tuple-element.110), channel_id=1, source_target_pairs={{0,6},{1,7},{2,4},{3,5},{4,2},{5,3},{6,0},{7,1},{8,14},{9,15},{10,... | collective-permute-start | bytes 86024 | tf_op jit(solution)/shard_map/ppermute | solution.py:507
  78.6 1.7 %collective-permute-start.27 = (bf16[112,128]{1,0:T(8,128)(2,1)S(1)}, bf16[112,128]{1,0:T(8,128)(2,1)S(1)}, u32[]{:S(2)}, u32[]{:S(2)}) collective-permute-start(bf16[112,128]{1,0:T(8,128)(2,1)S(1)} %get-tuple-element.111), channel_id=1, source_target_pairs={{0,4},{1,5},{2,6},{3,7},{4,0},{5,1},{6,2},{7,3},{8,12},{9,13},{10,... | collective-permute-start | bytes 86024 | tf_op jit(solution)/shard_map/ppermute | solution.py:507
  88.1 4.3 %collective-permute-done.32 = bf16[4,192,128]{2,1,0:T(8,128)(2,1)S(1)} collective-permute-done((bf16[4,192,128]{2,1,0:T(8,128)(2,1)S(1)}, bf16[4,192,128]{2,1,0:T(8,128)(2,1)S(1)}, u32[]{:S(2)}, u32[]{:S(2)}) %collective-permute-start.32) | collective-permute-done | bytes 196640 | tf_op jit(solution)/shard_map/ppermute | solution.py:507
  92.7 2.0 %collective-permute-start.35 = (bf16[336,128]{1,0:T(8,128)(2,1)S(1)}, bf16[336,128]{1,0:T(8,128)(2,1)S(1)}, u32[]{:S(2)}, u32[]{:S(2)}) collective-permute-start(bf16[336,128]{1,0:T(8,128)(2,1)S(1)} %get-tuple-element.103), channel_id=1, source_target_pairs={{0,6},{1,7},{2,4},{3,5},{4,2},{5,3},{6,0},{7,1},{8,14},{9,15},{10,... | collective-permute-start | bytes 258056 | tf_op jit(solution)/shard_map/ppermute | solution.py:507
  99.1 2.1 %collective-permute-done.34 = bf16[336,128]{1,0:T(8,128)(2,1)S(1)} collective-permute-done((bf16[336,128]{1,0:T(8,128)(2,1)S(1)}, bf16[336,128]{1,0:T(8,128)(2,1)S(1)}, u32[]{:S(2)}, u32[]{:S(2)}) %collective-permute-start.34) | collective-permute-done | bytes 86048 | tf_op jit(solution)/shard_map/ppermute | solution.py:507
  (154 shorter events, 25.5 us)
Async XLA Ops:
  1.8 9.8 %collective-permute-start.2 = (bf16[112,128]{1,0:T(8,128)(2,1)S(1)}, bf16[112,128]{1,0:T(8,128)(2,1)S(1)}, u32[]{:S(2)}, u32[]{:S(2)}) collective-permute-start(bf16[112,128]{1,0:T(8,128)(2,1)S(1)} %maximum_maximum_fusion), channel_id=1, source_target_pairs={{0,6},{1,7},{2,4},{3,5},{4,2},{5,3},{6,0},{7,1},{8,14},{9,15},{10,... | collective-permute-start | bytes 86024 | tf_op jit(solution)/shard_map/ppermute | solution.py:507
  6.9 8.2 %collective-permute-start.1 = (bf16[112,128]{1,0:T(8,128)(2,1)S(1)}, bf16[112,128]{1,0:T(8,128)(2,1)S(1)}, u32[]{:S(2)}, u32[]{:S(2)}) collective-permute-start(bf16[112,128]{1,0:T(8,128)(2,1)S(1)} %maximum_maximum_fusion), channel_id=1, source_target_pairs={{0,4},{1,5},{2,6},{3,7},{4,0},{5,1},{6,2},{7,3},{8,12},{9,13},{10,... | collective-permute-start | bytes 86024 | tf_op jit(solution)/shard_map/ppermute | solution.py:507
  6.9 8.2 %collective-permute-start = (bf16[112,128]{1,0:T(8,128)(2,1)S(1)}, bf16[112,128]{1,0:T(8,128)(2,1)S(1)}, u32[]{:S(2)}, u32[]{:S(2)}) collective-permute-start(bf16[112,128]{1,0:T(8,128)(2,1)S(1)} %maximum_maximum_fusion), channel_id=1, source_target_pairs={{0,2},{1,3},{2,0},{3,1},{4,6},{5,7},{6,4},{7,5},{8,10},{9,11},{10,... | collective-permute-start | bytes 86024 | tf_op jit(solution)/shard_map/ppermute | solution.py:507
  7.6 9.1 %collective-permute-start.9 = (bf16[336,128]{1,0:T(8,128)(2,1)S(1)}, bf16[336,128]{1,0:T(8,128)(2,1)S(1)}, u32[]{:S(2)}, u32[]{:S(2)}) collective-permute-start(bf16[336,128]{1,0:T(8,128)(2,1)S(1)} %pad_maximum_fusion.4), channel_id=1, source_target_pairs={{0,6},{1,7},{2,4},{3,5},{4,2},{5,3},{6,0},{7,1},{8,14},{9,15},{10,... | collective-permute-start | bytes 258056 | tf_op jit(solution)/shard_map/ppermute | solution.py:507
  11.5 6.9 %collective-permute-start.8 = (bf16[336,128]{1,0:T(8,128)(2,1)S(1)}, bf16[336,128]{1,0:T(8,128)(2,1)S(1)}, u32[]{:S(2)}, u32[]{:S(2)}) collective-permute-start(bf16[336,128]{1,0:T(8,128)(2,1)S(1)} %pad_maximum_fusion.4), channel_id=1, source_target_pairs={{0,4},{1,5},{2,6},{3,7},{4,0},{5,1},{6,2},{7,3},{8,12},{9,13},{10,... | collective-permute-start | bytes 258056 | tf_op jit(solution)/shard_map/ppermute | solution.py:507
  11.6 6.8 %collective-permute-start.7 = (bf16[336,128]{1,0:T(8,128)(2,1)S(1)}, bf16[336,128]{1,0:T(8,128)(2,1)S(1)}, u32[]{:S(2)}, u32[]{:S(2)}) collective-permute-start(bf16[336,128]{1,0:T(8,128)(2,1)S(1)} %pad_maximum_fusion.4), channel_id=1, source_target_pairs={{0,2},{1,3},{2,0},{3,1},{4,6},{5,7},{6,4},{7,5},{8,10},{9,11},{10,... | collective-permute-start | bytes 258056 | tf_op jit(solution)/shard_map/ppermute | solution.py:507
  15.2 6.6 %collective-permute-start.3 = (bf16[4,112,128]{2,1,0:T(8,128)(2,1)S(1)}, bf16[4,112,128]{2,1,0:T(8,128)(2,1)S(1)}, u32[]{:S(2)}, u32[]{:S(2)}) collective-permute-start(bf16[4,112,128]{2,1,0:T(8,128)(2,1)S(1)} %pad_maximum_fusion.3), channel_id=1, source_target_pairs={{0,1},{1,0},{2,3},{3,2},{4,5},{5,4},{6,7},{7,6},{8,9},{9,8},{10,11... | collective-permute-start | bytes 344072 | tf_op jit(solution)/shard_map/ppermute | solution.py:507
  18.4 7.2 %collective-permute-start.14 = (bf16[4,192,128]{2,1,0:T(8,128)(2,1)S(1)}, bf16[4,192,128]{2,1,0:T(8,128)(2,1)S(1)}, u32[]{:S(2)}, u32[]{:S(2)}) collective-permute-start(bf16[4,192,128]{2,1,0:T(8,128)(2,1)S(1)} %pad_maximum_fusion.1), channel_id=1, source_target_pairs={{0,16},{1,17},{2,18},{3,19},{4,20},{5,21},{6,22},{7,23},{8,24},{9,... | collective-permute-start | bytes 589832 | tf_op jit(solution)/shard_map/ppermute | solution.py:507
  20.0 7.8 %collective-permute-start.10 = (bf16[4,144,128]{2,1,0:T(8,128)(2,1)S(1)}, bf16[4,144,128]{2,1,0:T(8,128)(2,1)S(1)}, u32[]{:S(2)}, u32[]{:S(2)}) collective-permute-start(bf16[4,144,128]{2,1,0:T(8,128)(2,1)S(1)} %pad_maximum_fusion.2), channel_id=1, source_target_pairs={{0,1},{1,0},{2,3},{3,2},{4,5},{5,4},{6,7},{7,6},{8,9},{9,8},{10,11... | collective-permute-start | bytes 442376 | tf_op jit(solution)/shard_map/ppermute | solution.py:507
  21.8 8.8 %collective-permute-start.4 = (bf16[8,112,128]{2,1,0:T(8,128)(2,1)S(1)}, bf16[8,112,128]{2,1,0:T(8,128)(2,1)S(1)}, u32[]{:S(2)}, u32[]{:S(2)}) collective-permute-start(bf16[8,112,128]{2,1,0:T(8,128)(2,1)S(1)} %constant_dynamic-update-slice_fusion.refs_0_), channel_id=1, source_target_pairs={{0,16},{1,17},{2,18},{3,19},{4,20},{5,21},{6,22},{7,23},{8,24},{9,... | collective-permute-start | bytes 688136 | tf_op jit(solution)/shard_map/ppermute | solution.py:507
  25.6 9.8 %collective-permute-start.15 = (bf16[8,192,128]{2,1,0:T(8,128)(2,1)S(1)}, bf16[8,192,128]{2,1,0:T(8,128)(2,1)S(1)}, u32[]{:S(2)}, u32[]{:S(2)}) collective-permute-start(bf16[8,192,128]{2,1,0:T(8,128)(2,1)S(1)} %constant_dynamic-update-slice_fusion.10.refs_4_), channel_id=1, source_target_pairs={{0,1},{1,0},{2,3},{3,2},{4,5},{5,4},{6,7},{7,6},{8,9},{9,8},{10,11... | collective-permute-start | bytes 1179656 | tf_op jit(solution)/shard_map/ppermute | solution.py:507
  27.9 7.5 %collective-permute-start.11 = (bf16[8,144,128]{2,1,0:T(8,128)(2,1)S(1)}, bf16[8,144,128]{2,1,0:T(8,128)(2,1)S(1)}, u32[]{:S(2)}, u32[]{:S(2)}) collective-permute-start(bf16[8,144,128]{2,1,0:T(8,128)(2,1)S(1)} %constant_dynamic-update-slice_fusion.5.refs_0_), channel_id=1, source_target_pairs={{0,16},{1,17},{2,18},{3,19},{4,20},{5,21},{6,22},{7,23},{8,24},{9,... | collective-permute-start | bytes 884744 | tf_op jit(solution)/shard_map/ppermute | solution.py:507
  30.6 10.1 %collective-permute-start.12 = (bf16[8,144,128]{2,1,0:T(8,128)(2,1)S(1)}, bf16[8,144,128]{2,1,0:T(8,128)(2,1)S(1)}, u32[]{:S(2)}, u32[]{:S(2)}) collective-permute-start(bf16[8,144,128]{2,1,0:T(8,128)(2,1)S(1)} %constant_dynamic-update-slice_fusion.5.refs_0_), channel_id=1, source_target_pairs={{0,8},{1,9},{2,10},{3,11},{4,12},{5,13},{6,14},{7,15},{8,0},{9,1},... | collective-permute-start | bytes 884744 | tf_op jit(solution)/shard_map/ppermute | solution.py:507
  31.2 9.5 %collective-permute-start.16 = (bf16[8,192,128]{2,1,0:T(8,128)(2,1)S(1)}, bf16[8,192,128]{2,1,0:T(8,128)(2,1)S(1)}, u32[]{:S(2)}, u32[]{:S(2)}) collective-permute-start(bf16[8,192,128]{2,1,0:T(8,128)(2,1)S(1)} %constant_dynamic-update-slice_fusion.10.refs_4_), channel_id=1, source_target_pairs={{0,8},{1,9},{2,10},{3,11},{4,12},{5,13},{6,14},{7,15},{8,0},{9,1},... | collective-permute-start | bytes 1179656 | tf_op jit(solution)/shard_map/ppermute | solution.py:507
  62.7 14.1 %collective-permute-start.18 = (bf16[8,144,128]{2,1,0:T(8,128)(2,1)S(1)}, bf16[8,144,128]{2,1,0:T(8,128)(2,1)S(1)}, u32[]{:S(2)}, u32[]{:S(2)}) collective-permute-start(bf16[8,144,128]{2,1,0:T(8,128)(2,1)S(1)} %get-tuple-element.53), channel_id=1, source_target_pairs={{0,8},{1,9},{2,10},{3,11},{4,12},{5,13},{6,14},{7,15},{8,0},{9,1},... | collective-permute-start | bytes 884744 | tf_op jit(solution)/shard_map/ppermute | solution.py:507
  63.2 23.3 %collective-permute-start.29 = (bf16[8,192,128]{2,1,0:T(8,128)(2,1)S(1)}, bf16[8,192,128]{2,1,0:T(8,128)(2,1)S(1)}, u32[]{:S(2)}, u32[]{:S(2)}) collective-permute-start(bf16[8,192,128]{2,1,0:T(8,128)(2,1)S(1)} %get-tuple-element.70), channel_id=1, source_target_pairs={{0,8},{1,9},{2,10},{3,11},{4,12},{5,13},{6,14},{7,15},{8,0},{9,1},... | collective-permute-start | bytes 1179656 | tf_op jit(solution)/shard_map/ppermute | solution.py:507
  63.3 9.9 %collective-permute-start.30 = (bf16[8,192,128]{2,1,0:T(8,128)(2,1)S(1)}, bf16[8,192,128]{2,1,0:T(8,128)(2,1)S(1)}, u32[]{:S(2)}, u32[]{:S(2)}) collective-permute-start(bf16[8,192,128]{2,1,0:T(8,128)(2,1)S(1)} %get-tuple-element.72), channel_id=1, source_target_pairs={{0,8},{1,9},{2,10},{3,11},{4,12},{5,13},{6,14},{7,15},{8,0},{9,1},... | collective-permute-start | bytes 1179656 | tf_op jit(solution)/shard_map/ppermute | solution.py:507
  63.8 7.7 %collective-permute-start.24 = (bf16[8,112,128]{2,1,0:T(8,128)(2,1)S(1)}, bf16[8,112,128]{2,1,0:T(8,128)(2,1)S(1)}, u32[]{:S(2)}, u32[]{:S(2)}) collective-permute-start(bf16[8,112,128]{2,1,0:T(8,128)(2,1)S(1)} %add_convert_fusion.2), channel_id=1, source_target_pairs={{0,16},{1,17},{2,18},{3,19},{4,20},{5,21},{6,22},{7,23},{8,24},{9,... | collective-permute-start | bytes 688136 | tf_op jit(solution)/shard_map/ppermute | solution.py:507
  65.4 13.1 %collective-permute-start.20 = (bf16[8,144,128]{2,1,0:T(8,128)(2,1)S(1)}, bf16[8,144,128]{2,1,0:T(8,128)(2,1)S(1)}, u32[]{:S(2)}, u32[]{:S(2)}) collective-permute-start(bf16[8,144,128]{2,1,0:T(8,128)(2,1)S(1)} %add_convert_fusion.1), channel_id=1, source_target_pairs={{0,1},{1,0},{2,3},{3,2},{4,5},{5,4},{6,7},{7,6},{8,9},{9,8},{10,11... | collective-permute-start | bytes 884744 | tf_op jit(solution)/shard_map/ppermute | solution.py:507
  73.2 13.2 %collective-permute-start.31 = (bf16[8,192,128]{2,1,0:T(8,128)(2,1)S(1)}, bf16[8,192,128]{2,1,0:T(8,128)(2,1)S(1)}, u32[]{:S(2)}, u32[]{:S(2)}) collective-permute-start(bf16[8,192,128]{2,1,0:T(8,128)(2,1)S(1)} %add_convert_fusion), channel_id=1, source_target_pairs={{0,16},{1,17},{2,18},{3,19},{4,20},{5,21},{6,22},{7,23},{8,24},{9,... | collective-permute-start | bytes 1179656 | tf_op jit(solution)/shard_map/ppermute | solution.py:507
  76.8 5.7 %collective-permute-start.28 = (bf16[112,128]{1,0:T(8,128)(2,1)S(1)}, bf16[112,128]{1,0:T(8,128)(2,1)S(1)}, u32[]{:S(2)}, u32[]{:S(2)}) collective-permute-start(bf16[112,128]{1,0:T(8,128)(2,1)S(1)} %get-tuple-element.110), channel_id=1, source_target_pairs={{0,6},{1,7},{2,4},{3,5},{4,2},{5,3},{6,0},{7,1},{8,14},{9,15},{10,... | collective-permute-start | bytes 86024 | tf_op jit(solution)/shard_map/ppermute | solution.py:507
  86.6 5.7 %collective-permute-start.32 = (bf16[4,192,128]{2,1,0:T(8,128)(2,1)S(1)}, bf16[4,192,128]{2,1,0:T(8,128)(2,1)S(1)}, u32[]{:S(2)}, u32[]{:S(2)}) collective-permute-start(bf16[4,192,128]{2,1,0:T(8,128)(2,1)S(1)} %slice.200), channel_id=1, source_target_pairs={{0,1},{1,0},{2,3},{3,2},{4,5},{5,4},{6,7},{7,6},{8,9},{9,8},{10,11... | collective-permute-start | bytes 589832 | tf_op jit(solution)/shard_map/ppermute | solution.py:507
  92.7 6.4 %collective-permute-start.35 = (bf16[336,128]{1,0:T(8,128)(2,1)S(1)}, bf16[336,128]{1,0:T(8,128)(2,1)S(1)}, u32[]{:S(2)}, u32[]{:S(2)}) collective-permute-start(bf16[336,128]{1,0:T(8,128)(2,1)S(1)} %get-tuple-element.103), channel_id=1, source_target_pairs={{0,6},{1,7},{2,4},{3,5},{4,2},{5,3},{6,0},{7,1},{8,14},{9,15},{10,... | collective-permute-start | bytes 258056 | tf_op jit(solution)/shard_map/ppermute | solution.py:507
  94.8 6.5 %collective-permute-start.34 = (bf16[336,128]{1,0:T(8,128)(2,1)S(1)}, bf16[336,128]{1,0:T(8,128)(2,1)S(1)}, u32[]{:S(2)}, u32[]{:S(2)}) collective-permute-start(bf16[336,128]{1,0:T(8,128)(2,1)S(1)} %get-tuple-element.104), channel_id=1, source_target_pairs={{0,4},{1,5},{2,6},{3,7},{4,0},{5,1},{6,2},{7,3},{8,12},{9,13},{10,... | collective-permute-start | bytes 258056 | tf_op jit(solution)/shard_map/ppermute | solution.py:507
  (33 other events, 115.4 us)
